TPU v7x, 128 devices: a whole 4x4x4 slice. The times are simulated.
128 devices in a mesh: gx: 8 (over x, core), gy: 16 (over y, z).
Axes of the slice: x: 4, y: 4, z: 4, core: 2. Of those that a mesh axis runs over, the one named last changes fastest.
Arguments:
- coil_images: float32 [2, 2, 512, 256, 256], P(None, None, 'gx', 'gy'), may hold values from -6 to 6
- send_lists: int32 [128, 128, 4], P(('gx', 'gy')), may hold values from -1 to 65535, as said below
- seg_slots: int32 [2048, 16], P(('gx', 'gy')), may hold values from 0 to 511, as said below
- weights: float32 [2048, 16, 16, 512], P(('gx', 'gy')), may hold values from -0.0625 to 0.0625
- counts: int32 [2048], P(('gx', 'gy')), may hold values from 1 to 16
Outputs:
- kspace: float32 [2048, 2, 2, 16], P(('gx', 'gy'))
Inputs may be any that keep to these rules, and one draw needn't show every extreme that they name: Every entry of send_lists[d] that is not -1 names a grid block held by device d, with devices numbered x slab first: the block's x cells lie in device d's x cells and its y cells in device d's y cells. seg_slots[s, l] = j * 4 + k always names a slot with send_lists[j, s // 16, k] >= 0; the slots named by the segments of one owner are distinct, and every used slot of send_lists is named once.
All inputs are finite; a program needn't handle non-finite values.
Results may differ from a plain program's by a relative error of at most 0.00011.
Values sent between devices are 32-bit elements; how exact they have to be, the bound alone decides.
A program may use at most 256 MiB of HBM per device.

v0:
```python
import math

import jax
import jax.numpy as jnp
from jax import lax
from jax.sharding import PartitionSpec as P

BLOCK = 8


HIGHEST_PRECISION = lax.Precision.HIGHEST


def from_partner(block, axis, stride):
    count = lax.axis_size(axis)
    route = []
    for low in range(count):
        high = low | 1 << stride
        if high != low and high < count:
            route += [(low, high), (high, low)]
    return lax.ppermute(block, axis, route)


def dft_tables(length, norm_scale):
    freq_index = jnp.arange(length, dtype=jnp.int32)
    product = freq_index[:, None] * freq_index[None, :] % length
    phase_angle = product.astype(jnp.float32) * (2.0 * math.pi / length)
    return (jnp.cos(phase_angle) * norm_scale, jnp.sin(phase_angle) * norm_scale)


def combine_parts(cosine_part, sine_part):
    return jnp.stack([cosine_part[:, 0] + sine_part[:, 1], cosine_part[:, 1] - sine_part[:, 0]], 1)


def along_x(spectrum):
    cosine, sine = dft_tables(spectrum.shape[2], 1.0)
    cosine_part = jnp.einsum("km,cimyz->cikyz", cosine, spectrum, precision=HIGHEST_PRECISION)
    sine_part = jnp.einsum("km,cimyz->cikyz", sine, spectrum, precision=HIGHEST_PRECISION)
    return combine_parts(cosine_part, sine_part)


def along_y(spectrum):
    cosine, sine = dft_tables(spectrum.shape[3], 1.0)
    cosine_part = jnp.einsum("km,cixmz->cixkz", cosine, spectrum, precision=HIGHEST_PRECISION)
    sine_part = jnp.einsum("km,cixmz->cixkz", sine, spectrum, precision=HIGHEST_PRECISION)
    return combine_parts(cosine_part, sine_part)


def bit_reverse(value, bit_count):
    result = value * 0
    for bit_number in range(bit_count):
        result = result + jnp.left_shift(
            jnp.bitwise_and(jnp.right_shift(value, bit_number), 1), bit_count - 1 - bit_number
        )
    return result


def butterfly_step(own_part, partner, device_index, half_span):
    is_upper = jnp.bitwise_and(device_index, half_span) != 0
    flip_sign = jnp.where(is_upper, -1.0, 1.0).astype(jnp.float32)
    offset = jnp.bitwise_and(device_index, half_span - 1)
    phase_angle = offset.astype(jnp.float32) * (-math.pi / half_span)
    w_real = jnp.where(is_upper, jnp.cos(phase_angle), 1.0)
    w_imag = jnp.where(is_upper, jnp.sin(phase_angle), 0.0)
    summed = partner + flip_sign * own_part
    real_part = summed[:, 0]
    imag_part = summed[:, 1]
    return jnp.stack(
        [real_part * w_real - imag_part * w_imag, real_part * w_imag + imag_part * w_real], 1
    )


def twiddle(spectrum, dim, freq_low, total_length):
    rows = spectrum.shape[dim]
    row_index = jnp.arange(rows, dtype=jnp.int32)
    phase_index = row_index * freq_low % total_length
    phase_angle = phase_index.astype(jnp.float32) * (-2.0 * math.pi / total_length)
    shape_list = [1, 1, 1, 1]
    shape_list[dim - 1] = rows
    cosine = jnp.cos(phase_angle).reshape(shape_list)
    sine = jnp.sin(phase_angle).reshape(shape_list)
    real_part = spectrum[:, 0]
    imag_part = spectrum[:, 1]
    return jnp.stack(
        [real_part * cosine - imag_part * sine, real_part * sine + imag_part * cosine], 1
    )


def x_butterfly(spectrum):
    axis_count = lax.axis_size("gx")
    device_index = lax.axis_index("gx")
    bit_count = axis_count.bit_length() - 1
    for section_bit in range(bit_count - 1, -1, -1):
        partner = from_partner(spectrum, "gx", section_bit)
        spectrum = butterfly_step(spectrum, partner, device_index, 1 << section_bit)
    spectrum = twiddle(
        spectrum, 2, bit_reverse(device_index, bit_count), spectrum.shape[2] * axis_count
    )
    spectrum = along_x(spectrum)
    coil_count, part_count, rows_x, rows_y, z_cells = spectrum.shape
    pieces = spectrum.reshape(
        coil_count, part_count, axis_count, rows_x // axis_count, rows_y, z_cells
    )
    arrived = lax.all_to_all(pieces, "gx", split_axis=2, concat_axis=2, tiled=True)
    order_table = bit_reverse(jnp.arange(axis_count, dtype=jnp.int32), bit_count)
    arrived = jnp.take(arrived, order_table, axis=2)
    return jnp.swapaxes(arrived, 2, 3).reshape(coil_count, part_count, rows_x, rows_y, z_cells)


def y_butterfly(spectrum):
    axis_count = lax.axis_size("gy")
    device_index = lax.axis_index("gy")
    bit_count = axis_count.bit_length() - 1
    for section_bit in range(bit_count - 1, -1, -1):
        partner = from_partner(spectrum, "gy", section_bit)
        spectrum = butterfly_step(spectrum, partner, device_index, 1 << section_bit)
    spectrum = twiddle(
        spectrum, 3, bit_reverse(device_index, bit_count), spectrum.shape[3] * axis_count
    )
    spectrum = along_y(spectrum)
    coil_count, part_count, rows_x, rows_y, z_cells = spectrum.shape
    pieces = spectrum.reshape(
        coil_count, part_count, rows_x, axis_count, rows_y // axis_count, z_cells
    )
    arrived = lax.all_to_all(pieces, "gy", split_axis=3, concat_axis=3, tiled=True)
    order_table = bit_reverse(jnp.arange(axis_count, dtype=jnp.int32), bit_count)
    arrived = jnp.take(arrived, order_table, axis=3)
    return jnp.swapaxes(arrived, 3, 4).reshape(coil_count, part_count, rows_x, rows_y, z_cells)


def interpolate(spectrum, send_lists, seg_slots, weights, counts):
    coil_count, part_count, rows_x, rows_y, z_cells = spectrum.shape
    block_x = rows_x // BLOCK
    block_y = rows_y // BLOCK
    block_z = z_cells // BLOCK
    cell_count = BLOCK * BLOCK * BLOCK
    blocks = spectrum.reshape(
        coil_count, part_count, block_x, BLOCK, block_y, BLOCK, block_z, BLOCK
    )
    blocks = blocks.transpose(2, 4, 6, 0, 1, 3, 5, 7).reshape(
        block_x * block_y * block_z, coil_count * part_count * cell_count
    )
    global_y = rows_y * lax.axis_size("gy") // BLOCK
    clipped = jnp.maximum(send_lists[0], 0)
    block_z_index = clipped % block_z
    remainder = clipped // block_z
    block_y_index = remainder % global_y
    block_x_index = remainder // global_y
    local_id = (
        block_x_index % block_x * block_y + block_y_index % block_y
    ) * block_z + block_z_index
    sent_rows = jnp.take(blocks, local_id, axis=0)
    arrived = lax.all_to_all(sent_rows, ("gx", "gy"), split_axis=0, concat_axis=0, tiled=True)
    slot_rows = arrived.reshape(arrived.shape[0] * arrived.shape[1], arrived.shape[2])
    seg_count, list_len = seg_slots.shape
    picked = jnp.take(slot_rows, seg_slots.reshape(-1), axis=0)
    picked = picked.reshape(seg_count, list_len, coil_count * part_count, cell_count)
    samples = jnp.einsum("slnk,slqk->sqn", weights, picked, precision=HIGHEST_PRECISION)
    live_mask = jnp.arange(samples.shape[2], dtype=jnp.int32)[None, None, :] < counts[:, None, None]
    samples = jnp.where(live_mask, samples, jnp.zeros_like(samples))
    return samples.reshape(seg_count, coil_count, part_count, samples.shape[2])


def local(coil_images, send_lists, seg_slots, weights, counts):
    total_cells = (
        coil_images.shape[2]
        * lax.axis_size("gx")
        * coil_images.shape[3]
        * lax.axis_size("gy")
        * coil_images.shape[4]
    )
    cosine, sine = dft_tables(coil_images.shape[4], 1.0 / math.sqrt(total_cells))
    cosine_part = jnp.matmul(coil_images, cosine, precision=HIGHEST_PRECISION)
    sine_part = jnp.matmul(coil_images, sine, precision=HIGHEST_PRECISION)
    spectrum = combine_parts(cosine_part, sine_part)
    spectrum = x_butterfly(spectrum)
    spectrum = y_butterfly(spectrum)
    return interpolate(spectrum, send_lists, seg_slots, weights, counts)


def solution(mesh):
    placed = (
        P(None, None, "gx", "gy", None),
        P(("gx", "gy"), None, None),
        P(("gx", "gy"), None),
        P(("gx", "gy"), None, None, None),
        P(("gx", "gy")),
    )
    return jax.shard_map(
        local,
        mesh=mesh,
        in_specs=placed,
        out_specs=P(("gx", "gy"), None, None, None),
        check_vma=False,
    )
```

profile of v0, /device:TPU:1, one launch (start us, length us, event | category | flops | bytes accessed | tf_op | source)
XLA Modules:
  0.0 1066.1 jit_solution(5013093389736763282)
XLA Ops:
  0.0 10.5 fusion.12
  10.6 6.5 fusion.15
  24.5 90.0 %collective-permute-done = f32[2,2,64,16,256]{4,2,3,1,0:T(8,128)} collective-permute-done((f32[2,2,64,16,256]{4,2,3,1,0:T(8,128)}, f32[2,2,64,16,256]{4,2,3,1,0:T(8,128)}, u32[]{:S(2)}, u32[]{:S(2)}) %collective-permute-start) | collective-permute-done | bytes 4194336 | tf_op jit(solution)/shard_map/ppermute | solution.py:21
  123.2 89.2 %collective-permute-done.1 = f32[2,2,64,16,256]{4,2,3,1,0:T(8,128)} collective-permute-done((f32[2,2,64,16,256]{4,2,3,1,0:T(8,128)}, f32[2,2,64,16,256]{4,2,3,1,0:T(8,128)}, u32[]{:S(2)}, u32[]{:S(2)}) %collective-permute-start.1) | collective-permute-done | bytes 4194336 | tf_op jit(solution)/shard_map/ppermute | solution.py:21
  222.1 7.1 collective-permute-done.2
  252.1 48.8 %all-to-all-done = f32[2,2,8,8,16,256]{5,3,4,0,1,2:T(8,128)} async-done(((f32[2,2,8,8,16,256]{5,3,4,0,1,2:T(8,128)}), f32[2,2,8,8,16,256]{5,3,4,0,1,2:T(8,128)}, u32[]{:S(2)}, u32[]{:S(2)}) %all-to-all-start) | async-done | bytes 4194336 | tf_op jit(solution)/shard_map/all_to_all | solution.py:104
  315.1 90.0 %collective-permute-done.3 = f32[2,2,64,16,256]{4,3,2,1,0:T(8,128)} collective-permute-done((f32[2,2,64,16,256]{4,3,2,1,0:T(8,128)}, f32[2,2,64,16,256]{4,3,2,1,0:T(8,128)}, u32[]{:S(2)}, u32[]{:S(2)}) %collective-permute-start.3) | collective-permute-done | bytes 4194336 | tf_op jit(solution)/shard_map/ppermute | solution.py:21
  414.3 89.3 %collective-permute-done.4 = f32[2,2,64,16,256]{4,3,2,1,0:T(8,128)} collective-permute-done((f32[2,2,64,16,256]{4,3,2,1,0:T(8,128)}, f32[2,2,64,16,256]{4,3,2,1,0:T(8,128)}, u32[]{:S(2)}, u32[]{:S(2)}) %collective-permute-start.4) | collective-permute-done | bytes 4194336 | tf_op jit(solution)/shard_map/ppermute | solution.py:21
  514.4 88.3 %collective-permute-done.5 = f32[2,2,64,16,256]{4,3,2,1,0:T(8,128)} collective-permute-done((f32[2,2,64,16,256]{4,3,2,1,0:T(8,128)}, f32[2,2,64,16,256]{4,3,2,1,0:T(8,128)}, u32[]{:S(2)}, u32[]{:S(2)}) %collective-permute-start.5) | collective-permute-done | bytes 4194336 | tf_op jit(solution)/shard_map/ppermute | solution.py:21
  610.8 88.3 %collective-permute-done.6 = f32[2,2,64,16,256]{4,3,2,1,0:T(8,128)} collective-permute-done((f32[2,2,64,16,256]{4,3,2,1,0:T(8,128)}, f32[2,2,64,16,256]{4,3,2,1,0:T(8,128)}, u32[]{:S(2)}, u32[]{:S(2)}) %collective-permute-start.6) | collective-permute-done | bytes 4194336 | tf_op jit(solution)/shard_map/ppermute | solution.py:21
  718.2 6.8 all-to-all-start.1
  725.4 47.5 %all-to-all-done.1 = f32[2,2,64,16,1,256]{5,2,1,0,4,3:T(8,128)} async-done(((f32[2,2,64,16,1,256]{5,2,1,0,4,3:T(8,128)}), f32[2,2,64,16,1,256]{5,2,1,0,4,3:T(8,128)}, u32[]{:S(2)}, u32[]{:S(2)}) %all-to-all-start.1) | async-done | bytes 4194336 | tf_op jit(solution)/shard_map/all_to_all | solution.py:125
  782.6 6.6 copy.28
  789.2 42.0 %gather.22 = f32[2,2,8,8,2,8,32,8]{7,6,5,4,3,2,1,0:T(8,128)} reshape(f32[2,2,64,16,256]{4,3,2,1,0:T(8,128)} %copy.28) | data formatting | bytes 8388608 | tf_op jit(solution)/shard_map/jit(_take)/gather | solution.py:127
  831.2 44.8 %select_bitcast_fusion = f32[8,2,32,2,2,8,8,8]{7,2,6,1,5,0,4,3:T(8,128)} fusion(f32[2,2,8,8,2,8,32,8]{7,6,5,4,3,2,1,0:T(8,128)} %gather.22, pred[2,8]{1,0:T(4,128)(4,1)S(1)} %compare_and_fusion.2), kind=kLoop, calls=%fused_computation.4 | loop fusion | flops 1048576 | bytes 8388624 | tf_op jit(solution)/shard_map/transpose | solution.py:140
  876.0 50.6 %copy.29 = f32[8,2,32,2,2,8,8,8]{2,1,0,7,6,5,4,3:T(2,128)} copy(f32[8,2,32,2,2,8,8,8]{7,2,6,1,5,0,4,3:T(8,128)} %select_bitcast_fusion) | data formatting | bytes 8388608 | tf_op jit(solution)/shard_map/transpose | solution.py:140
  926.6 21.7 %reshape.490 = f32[512,2048]{0,1:T(8,128)} reshape(f32[8,2,32,2,2,8,8,8]{2,1,0,7,6,5,4,3:T(2,128)} %copy.29) | data formatting | bytes 8388608 | tf_op jit(solution)/shard_map/reshape | solution.py:140
  948.3 5.5 copy.31
  953.7 7.6 gather_fusion.2
  961.3 5.5 reshape.513
  972.0 14.3 %all-to-all-start.2 = ((f32[128,4,2048]{2,1,0:T(4,128)}), f32[128,4,2048]{2,1,0:T(4,128)}, u32[]{:S(2)}, u32[]{:S(2)}) async-start(f32[128,4,2048]{2,1,0:T(4,128)} %broadcast_select_fusion), calls=%async_computation.2 | async-start | bytes 8388608 | tf_op jit(solution)/shard_map/all_to_all | solution.py:153
  986.6 51.8 %all-to-all-done.2 = f32[128,4,2048]{2,1,0:T(4,128)} async-done(((f32[128,4,2048]{2,1,0:T(4,128)}), f32[128,4,2048]{2,1,0:T(4,128)}, u32[]{:S(2)}, u32[]{:S(2)}) %all-to-all-start.2) | async-done | bytes 4194336 | tf_op jit(solution)/shard_map/all_to_all | solution.py:153
  1043.8 5.8 gather_fusion.3
  1052.3 13.4 %fusion.25 = f32[16,4,16]{2,1,0:T(4,128)} fusion(f32[16,16,16,512]{3,2,1,0:T(8,128)} %param.8, f32[16,16,4,512]{3,2,1,0:T(4,128)S(1)} %gather.25, pred[16,16]{1,0:T(8,128)(4,1)S(1)} %get-tuple-element.30, pred[16,16]{1,0:T(8,128)(4,1)S(1)} %get-tuple-element.29), kind=kOutput, calls=%fused_computation.68 | convolution fusion | flops 101188608 | bytes 10490368 | tf_op jit(solution)/shard_map/slnk,slqk->sqn/dot_general | solution.py:158
  (85 shorter events, 132.7 us)
Async XLA Ops:
  0.0 10.5 copy-start.6
  18.0 2.6 copy-start.5
  20.6 93.9 %collective-permute-start = (f32[2,2,64,16,256]{4,2,3,1,0:T(8,128)}, f32[2,2,64,16,256]{4,2,3,1,0:T(8,128)}, u32[]{:S(2)}, u32[]{:S(2)}) collective-permute-start(f32[2,2,64,16,256]{4,2,3,1,0:T(8,128)} %pad_maximum_fusion), channel_id=1, source_target_pairs={{0,64},{64,0},{16,80},{80,16},{32,96},{96,32},{48,112},{112,48},{1... | collective-permute-start | bytes 12582920 | tf_op jit(solution)/shard_map/ppermute | solution.py:21
  118.8 2.7 copy-start.4
  121.5 90.9 %collective-permute-start.1 = (f32[2,2,64,16,256]{4,2,3,1,0:T(8,128)}, f32[2,2,64,16,256]{4,2,3,1,0:T(8,128)}, u32[]{:S(2)}, u32[]{:S(2)}) collective-permute-start(f32[2,2,64,16,256]{4,2,3,1,0:T(8,128)} %pad_maximum_fusion.1), channel_id=1, source_target_pairs={{0,32},{32,0},{16,48},{48,16},{64,96},{96,64},{80,112},{112,80},{1... | collective-permute-start | bytes 12582920 | tf_op jit(solution)/shard_map/ppermute | solution.py:21
  216.7 2.7 copy-start.1
  219.4 9.8 collective-permute-start.2
  246.7 54.2 %all-to-all-start = ((f32[2,2,8,8,16,256]{5,3,4,0,1,2:T(8,128)}), f32[2,2,8,8,16,256]{5,3,4,0,1,2:T(8,128)}, u32[]{:S(2)}, u32[]{:S(2)}) async-start(f32[2,2,8,8,16,256]{5,3,4,0,1,2:T(8,128)} %copy.39), calls=%async_computation | async-start | bytes 8388608 | tf_op jit(solution)/shard_map/all_to_all | solution.py:104
  311.9 93.2 %collective-permute-start.3 = (f32[2,2,64,16,256]{4,3,2,1,0:T(8,128)}, f32[2,2,64,16,256]{4,3,2,1,0:T(8,128)}, u32[]{:S(2)}, u32[]{:S(2)}) collective-permute-start(f32[2,2,64,16,256]{4,3,2,1,0:T(8,128)} %bitcast.19), channel_id=1, source_target_pairs={{0,8},{8,0},{1,9},{9,1},{2,10},{10,2},{3,11},{11,3},{4,12},{12,4},... | collective-permute-start | bytes 12582920 | tf_op jit(solution)/shard_map/ppermute | solution.py:21
  410.2 2.6 copy-start.2
  412.9 90.7 %collective-permute-start.4 = (f32[2,2,64,16,256]{4,3,2,1,0:T(8,128)}, f32[2,2,64,16,256]{4,3,2,1,0:T(8,128)}, u32[]{:S(2)}, u32[]{:S(2)}) collective-permute-start(f32[2,2,64,16,256]{4,3,2,1,0:T(8,128)} %pad_maximum_fusion.5), channel_id=1, source_target_pairs={{0,4},{4,0},{1,5},{5,1},{2,6},{6,2},{3,7},{7,3},{8,12},{12,8},{9,1... | collective-permute-start | bytes 12582920 | tf_op jit(solution)/shard_map/ppermute | solution.py:21
  508.1 2.6 copy-start.3
  510.7 92.0 %collective-permute-start.5 = (f32[2,2,64,16,256]{4,3,2,1,0:T(8,128)}, f32[2,2,64,16,256]{4,3,2,1,0:T(8,128)}, u32[]{:S(2)}, u32[]{:S(2)}) collective-permute-start(f32[2,2,64,16,256]{4,3,2,1,0:T(8,128)} %pad_maximum_fusion.6), channel_id=1, source_target_pairs={{0,2},{2,0},{1,3},{3,1},{4,6},{6,4},{5,7},{7,5},{8,10},{10,8},{9,1... | collective-permute-start | bytes 12582920 | tf_op jit(solution)/shard_map/ppermute | solution.py:21
  607.3 2.6 copy-start
  609.9 89.2 %collective-permute-start.6 = (f32[2,2,64,16,256]{4,3,2,1,0:T(8,128)}, f32[2,2,64,16,256]{4,3,2,1,0:T(8,128)}, u32[]{:S(2)}, u32[]{:S(2)}) collective-permute-start(f32[2,2,64,16,256]{4,3,2,1,0:T(8,128)} %pad_maximum_fusion.7), channel_id=1, source_target_pairs={{0,1},{1,0},{2,3},{3,2},{4,5},{5,4},{6,7},{7,6},{8,9},{9,8},{10,11... | collective-permute-start | bytes 12582920 | tf_op jit(solution)/shard_map/ppermute | solution.py:21
  718.2 6.8 copy-start.8
  718.2 54.8 %all-to-all-start.1 = ((f32[2,2,64,16,1,256]{5,2,1,0,4,3:T(8,128)}), f32[2,2,64,16,1,256]{5,2,1,0,4,3:T(8,128)}, u32[]{:S(2)}, u32[]{:S(2)}) async-start(f32[2,2,64,16,1,256]{5,2,1,0,4,3:T(8,128)} %copy.26), calls=%async_computation.1 | async-start | bytes 8388608 | tf_op jit(solution)/shard_map/all_to_all | solution.py:125
  972.0 14.4 %copy-start.7 = (s32[16,16]{1,0:T(8,128)S(1)}, s32[16,16]{1,0:T(8,128)}, u32[]{:S(2)}) copy-start(s32[16,16]{1,0:T(8,128)} %param.7) | copy-start | bytes 3076
  972.0 14.5 %copy-start.9 = (s32[16]{0:T(128)S(1)}, s32[16]{0:T(128)}, u32[]{:S(2)}) copy-start(s32[16]{0:T(128)} %param.9) | copy-start | bytes 196
  972.0 66.3 %all-to-all-start.2 = ((f32[128,4,2048]{2,1,0:T(4,128)}), f32[128,4,2048]{2,1,0:T(4,128)}, u32[]{:S(2)}, u32[]{:S(2)}) async-start(f32[128,4,2048]{2,1,0:T(4,128)} %broadcast_select_fusion), calls=%async_computation.2 | async-start | bytes 8388608 | tf_op jit(solution)/shard_map/all_to_all | solution.py:153
where the time goes:
time: 1080 us; the launch traced here: 1070 us
  waiting for transfers between devices  690 us (64%)
  local copies, waits for them, and re-layouts  179 us (17%)
  other arithmetic  104 us (10%)
  matrix products  47.3 us (4%)
  starting transfers between devices  43.1 us (4%)
    ppermute x7, waiting for transfers between devices, from_partner(): return lax.ppermute(block, axis, route)  542 us
    gather x3, local copies, waits for them, and re-layouts, y_butterfly(): arrived = jnp.take(arrived, order_table, axis=3)  53.5 us
    all_to_all x1, waiting for transfers between devices, interpolate(): lax.all_to_all(sent_rows, ('gx', 'gy'), split_axis=0, concat_axis=0, tile...  51.8 us
    transpose x1, local copies, waits for them, and re-layouts, interpolate(): blocks.transpose(2, 4, 6, 0, 1, 3, 5, 7)  50.6 us
    all_to_all x1, waiting for transfers between devices, x_butterfly(): lax.all_to_all(pieces, 'gx', split_axis=2, concat_axis=2, tiled=True)  48.8 us
    all_to_all x1, waiting for transfers between devices, y_butterfly(): lax.all_to_all(pieces, 'gy', split_axis=3, concat_axis=3, tiled=True)  47.5 us
    transpose x1, other arithmetic, interpolate(): blocks.transpose(2, 4, 6, 0, 1, 3, 5, 7)  44.8 us
    add x7, other arithmetic, butterfly_step(): summed = partner + flip_sign * own_part  27.3 us
  transfers between devices with their start and end apart: 10, of which 10 were waited for; matrix products, arithmetic and copies ran while one was open for 0% of the time, Pallas kernels for 0%

commit v1 on v0

v1 whole, which is shorter than its diff:
```python
import functools
import math

import jax
import jax.numpy as jnp
import numpy as np
from jax import lax
from jax.experimental import pallas as pl
from jax.experimental.pallas import tpu as pltpu
from jax.sharding import PartitionSpec as P

NX, NY, NZ = 512, 256, 256
GX, GY = 8, 16
DEVS = GX * GY
F32, BF16 = jnp.float32, jnp.bfloat16
VMEM_LIMIT = 48 * 2**20


def split_table(table):
    hi = table.astype(np.float32).astype(jnp.bfloat16)
    lo = (table - hi.astype(np.float64)).astype(np.float32).astype(jnp.bfloat16)
    return hi, lo


def angle(rows, columns, length):
    return (np.outer(rows, columns) % length) * (2.0 * math.pi / length)


def z_table():
    order = (np.arange(8)[:, None] + 8 * np.arange(32)[None, :]).reshape(-1)
    phase = angle(order, np.arange(NZ), NZ)
    scale = 1.0 / math.sqrt(NX * NY * NZ)
    return split_table(np.concatenate([np.cos(phase), np.sin(phase)], 1) * scale)


def x_table():
    phase = angle(np.arange(NX), np.arange(NX), NX)
    cos, sin = np.cos(phase), np.sin(phase)
    whole = np.zeros((2, NX, 2, NX))
    whole[0, :, 0], whole[1, :, 0] = cos, sin
    whole[0, :, 1], whole[1, :, 1] = -sin, cos
    whole = whole.reshape(2, 8, 64, 2, 64, 8).transpose(1, 0, 2, 5, 3, 4)
    return split_table(whole.reshape(1024, 1024))


def y_table():
    phase = angle(np.arange(NY), np.arange(NY), NY)
    return split_table(np.concatenate([np.cos(phase), np.sin(phase)], 1))


def halves(value):
    hi = value.astype(BF16)
    return hi, (value - hi.astype(F32)).astype(BF16)


def dot3(left, right, dims):
    def one(a, b):
        return lax.dot_general(a, b, (dims, ((), ())), preferred_element_type=F32)

    return one(left[0], right[0]) + (one(left[0], right[1]) + one(left[1], right[0]))


def z_kernel(near, far, hi, lo, out):
    def pair(yp, carry):
        rows, swapped = [], []
        for k in range(2):
            at = pl.ds(2 * yp + k, 64, stride=16)
            re, im = (jnp.concatenate([near[0, q, at, :], far[0, q, at, :]], 1) for q in range(2))
            rows += [re, im]
            swapped += [im, -re]
        data = jnp.concatenate(
            [jnp.concatenate(rows, 0), jnp.concatenate(swapped, 0)], 1
        )
        res = dot3((hi[...], lo[...]), halves(data), ((1,), (1,)))
        for k in range(2):
            out[:, 0, 2 * yp + k] = res[:, k * 128 : (k + 1) * 128].reshape(8, 32, 128)
        return carry

    lax.fori_loop(0, 8, pair, 0)


def z_transform(images):
    images = images.reshape(2, 2, 1024, 256)
    hi, lo = z_table()
    whole = pl.BlockSpec((256, 512), lambda c: (0, 0))
    return pl.pallas_call(
        z_kernel,
        out_shape=jax.ShapeDtypeStruct((8, 2, 16, 32, 128), F32),
        grid=(2,),
        in_specs=[
            pl.BlockSpec((1, 2, 1024, 128), lambda c: (c, 0, 0, 0)),
            pl.BlockSpec((1, 2, 1024, 128), lambda c: (c, 0, 0, 1)),
            whole,
            whole,
        ],
        out_specs=pl.BlockSpec((8, 1, 16, 32, 128), lambda c: (0, c, 0, 0, 0)),
        compiler_params=pltpu.CompilerParams(vmem_limit_bytes=VMEM_LIMIT),
        name="z_transform",
    )(images, images, jnp.asarray(hi), jnp.asarray(lo))


def x_kernel(data, hi, lo, out):
    rows = jnp.concatenate([data[a] for a in range(8)], 1)
    res = dot3(halves(rows), (hi[...], lo[...]), ((1,), (0,)))
    for u in range(8):
        out[u] = res[:, u * 128 : (u + 1) * 128]


def x_transform(data):
    hi, lo = x_table()
    whole = pl.BlockSpec((1024, 1024), lambda r: (0, 0))
    return pl.pallas_call(
        x_kernel,
        out_shape=jax.ShapeDtypeStruct((16, 512, 128), F32),
        grid=(4,),
        in_specs=[pl.BlockSpec((8, 256, 128), lambda r: (0, r, 0)), whole, whole],
        out_specs=pl.BlockSpec((8, 256, 128), lambda r: (r // 2, r % 2, 0)),
        compiler_params=pltpu.CompilerParams(vmem_limit_bytes=VMEM_LIMIT),
        name="x_transform",
    )(data, jnp.asarray(hi), jnp.asarray(lo))


def y_kernel(data, hi, lo, out):
    flat = data.reshape(2048, 128)
    sign = jnp.where(lax.broadcasted_iota(jnp.int32, (256, 128), 1) < 64, 1.0, -1.0)

    def pair(p, carry):
        rows, swapped = [], []
        for k in range(2):
            part = flat[pl.ds(2 * p + k, 256, stride=8), :]
            rows.append(part)
            swapped.append(pltpu.roll(part, 64, 1) * sign)
        both = jnp.concatenate(
            [jnp.concatenate(rows, 1), jnp.concatenate(swapped, 1)], 0
        )
        res = dot3((hi[...], lo[...]), halves(both), ((1,), (0,)))
        for k in range(2):
            out[:, 2 * p + k] = res[:, k * 128 : (k + 1) * 128].reshape(32, 8, 128)
        return carry

    lax.fori_loop(0, 4, pair, 0)


def y_transform(data):
    hi, lo = y_table()
    whole = pl.BlockSpec((256, 512), lambda g: (0, 0))
    return pl.pallas_call(
        y_kernel,
        out_shape=jax.ShapeDtypeStruct((32, 32, 8, 128), F32),
        grid=(4,),
        in_specs=[pl.BlockSpec((256, 8, 128), lambda g: (0, g, 0)), whole, whole],
        out_specs=pl.BlockSpec((32, 8, 8, 128), lambda g: (0, g, 0, 0)),
        compiler_params=pltpu.CompilerParams(vmem_limit_bytes=VMEM_LIMIT),
        name="y_transform",
    )(data.reshape(256, 32, 128), jnp.asarray(hi), jnp.asarray(lo))


def pick_kernel(ids, table, out):
    lane = jnp.bitwise_and(lax.broadcasted_iota(jnp.int32, (8, 128), 1), 63)

    def group(t, carry):
        chains = [None] * 4
        for i in range(64):
            block = ids[t * 64 + i]
            tile = table[jnp.bitwise_and(block, 1023)]
            shift = jnp.bitwise_and(i - jnp.right_shift(block, 10), 127)
            moved = pltpu.roll(tile, shift, 1)
            old = chains[i % 4]
            chains[i % 4] = moved if old is None else jnp.where(lane == i, moved, old)
        low = jnp.bitwise_and(lane, 3)
        out[t] = jnp.where(
            low < 2,
            jnp.where(low == 0, chains[0], chains[1]),
            jnp.where(low == 2, chains[2], chains[3]),
        )
        return carry

    lax.fori_loop(0, 32, group, 0)


def pick(ids, table):
    return pl.pallas_call(
        pick_kernel,
        out_shape=jax.ShapeDtypeStruct((512, 8, 128), F32),
        grid=(16,),
        in_specs=[
            pl.BlockSpec((2048,), lambda g: (g,), memory_space=pltpu.SMEM),
            pl.BlockSpec((1024, 8, 128), lambda g: (0, 0, 0)),
        ],
        out_specs=pl.BlockSpec((32, 8, 128), lambda g: (g, 0, 0)),
        compiler_params=pltpu.CompilerParams(vmem_limit_bytes=VMEM_LIMIT),
        name="pick",
    )(ids, table.reshape(1024, 8, 128))


def turn_kernel(weights, out):
    def one(n, carry):
        out[0, n] = weights[0, pl.ds(n, 128, stride=16), :].T
        return carry

    lax.fori_loop(0, 16, one, 0)


def turn_weights(weights):
    return pl.pallas_call(
        turn_kernel,
        out_shape=jax.ShapeDtypeStruct((2, 16, 512, 128), F32),
        grid=(2, 4),
        in_specs=[pl.BlockSpec((1, 2048, 128), lambda h, e: (h, 0, e))],
        out_specs=pl.BlockSpec((1, 16, 128, 128), lambda h, e: (h, 0, e, 0)),
        compiler_params=pltpu.CompilerParams(vmem_limit_bytes=VMEM_LIMIT),
        name="turn_weights",
    )(weights.reshape(2, 2048, 512))


def sum_kernel(got, weights, out):
    low = lax.broadcasted_iota(jnp.int32, (8, 128), 1) < 64

    def one(t, carry):
        w, u = t // 8, t % 8
        values = []
        for c in range(2):
            first, second = got[w, c, u, 0], got[w, c, u, 1]
            values.append(jnp.where(low, first, pltpu.roll(second, 64, 1)))
            values.append(jnp.where(low, pltpu.roll(first, 64, 1), second))
        sums = list(carry)
        for n in range(4):
            factor = weights[0, n, pl.ds(u * 64 + w, 8, stride=8), :]
            for k in range(4):
                sums[n * 4 + k] = sums[n * 4 + k] + factor * values[k]
        return tuple(sums)

    sums = lax.fori_loop(0, 64, one, (jnp.zeros((8, 128), F32),) * 16)
    rows = [jnp.sum(s, 0, keepdims=True) for s in sums]
    out[0, 0] = jnp.concatenate(rows, 0)


def interpolate(got, weights):
    return pl.pallas_call(
        sum_kernel,
        out_shape=jax.ShapeDtypeStruct((2, 4, 16, 128), F32),
        grid=(2, 4),
        in_specs=[
            pl.BlockSpec((8, 2, 8, 2, 8, 128), lambda h, n: (0, 0, 0, h, 0, 0)),
            pl.BlockSpec((1, 4, 512, 128), lambda h, n: (h, n, 0, 0)),
        ],
        out_specs=pl.BlockSpec((1, 1, 16, 128), lambda h, n: (h, n, 0, 0)),
        compiler_params=pltpu.CompilerParams(vmem_limit_bytes=VMEM_LIMIT),
        name="interpolate",
    )(got, weights)


def block_ids(send_lists, seg_slots):
    both = ("gx", "gy")
    lists = lax.all_to_all(send_lists[0], both, 0, 0, tiled=True).reshape(1, 512)
    hit = seg_slots.reshape(256, 1) == jnp.arange(512, dtype=jnp.int32)[None, :]
    ids = jnp.sum(jnp.where(hit, lists, 0), 1)
    return lax.all_gather(ids, both, axis=0, tiled=True)


def local(coil_images, send_lists, seg_slots, weights, counts):
    ids = block_ids(send_lists, seg_slots)
    turned = turn_weights(weights)
    spectrum = z_transform(coil_images).reshape(8, 1024, 128)
    spectrum = lax.all_to_all(spectrum, "gx", 0, 0, tiled=True)
    spectrum = x_transform(spectrum)
    spectrum = lax.all_to_all(spectrum, "gy", 0, 0, tiled=True)
    table = y_transform(spectrum)
    sent = pick(ids, table).reshape(128, 4, 8, 128)
    got = lax.all_to_all(sent, ("gx", "gy"), 0, 0, tiled=True)
    sums = interpolate(got.reshape(8, 2, 8, 4, 8, 128), turned)
    sums = sums.reshape(2, 16, 2, 2, 8, 16).sum(-1)
    samples = sums.transpose(0, 4, 2, 3, 1).reshape(16, 2, 2, 16)
    live = jnp.arange(16, dtype=jnp.int32) < counts[:, None, None, None]
    return jnp.where(live, samples, 0.0)


def solution(mesh):
    placed = (
        P(None, None, "gx", "gy", None),
        P(("gx", "gy"), None, None),
        P(("gx", "gy"), None),
        P(("gx", "gy"), None, None, None),
        P(("gx", "gy")),
    )
    return jax.shard_map(
        local,
        mesh=mesh,
        in_specs=placed,
        out_specs=P(("gx", "gy"), None, None, None),
        check_vma=False,
    )
```

time: 1080 us -> 401 us (0.37); the launches traced: 1070 us -> 400 us
  waiting for transfers between devices: 690 us -> 62.1 us
  Pallas kernels: 0 us -> 191 us
  local copies, waits for them, and re-layouts: 179 us -> 11.1 us
  blocking collectives: 0 us -> 106 us
  other arithmetic: 104 us -> 1.35 us
  matrix products: 47.3 us -> 0 us
  starting transfers between devices: 43.1 us -> 28.5 us
    ppermute x7 -> x0, waiting for transfers between devices: 542 us -> none  [from_partner(): return lax.ppermute(block, axis, route)]
    pallas_call x0 -> x6, Pallas kernels: none -> 191 us  [the longest x1 106 us: pick(): pl.pallas_call(pick_kernel, out_shape=jax.ShapeDtypeStruct((512, 8, 128),...]
    all_gather x0 -> x1, blocking collectives: none -> 106 us  [block_ids(): return lax.all_gather(ids, both, axis=0, tiled=True)]
    all_to_all x3 -> x4, waiting for transfers between devices: 148 us -> 62.1 us  [the longest x1 48.2 us: local(): spectrum = lax.all_to_all(spectrum, 'gx', 0, 0, tiled=True)]
    gather x8 -> x0, local copies, waits for them, and re-layouts: 80.1 us -> none  [the longest x3 53.5 us: y_butterfly(): arrived = jnp.take(arrived, order_table, axis=3)]
    transpose x1, local copies, waits for them, and re-layouts: 50.6 us -> 0.08 us  [local(): samples = sums.transpose(0, 4, 2, 3, 1).reshape(16, 2, 2, 16)]
    dot_general x7 -> x0, matrix products: 47.3 us -> none  [the longest x1 13.4 us: interpolate(): jnp.einsum('slnk,slqk->sqn', weights, picked, precision=HIGHEST_PRECISION)]
    transpose x1 -> x0, other arithmetic: 44.8 us -> none  [interpolate(): blocks.transpose(2, 4, 6, 0, 1, 3, 5, 7)]
  transfers between devices with their start and end apart: 10 -> 4, of which waited for: 10 -> 2; matrix products, arithmetic and copies ran while one was open for 0% -> 1% of each run, Pallas kernels for 0% -> 6%
where the time goes in v1:
time: 401 us; the launch traced here: 400 us
  Pallas kernels  191 us (48%)
  blocking collectives  106 us (26%)
  waiting for transfers between devices  62.1 us (15%)
  starting transfers between devices  28.5 us (7%)
  local copies, waits for them, and re-layouts  11.1 us (3%)
    all_gather x1, blocking collectives, block_ids(): return lax.all_gather(ids, both, axis=0, tiled=True)  106 us
    pallas_call x1, Pallas kernels, pick(): pl.pallas_call(pick_kernel, out_shape=jax.ShapeDtypeStruct((512, 8, 128),...  106 us
    all_to_all x1, waiting for transfers between devices, local(): spectrum = lax.all_to_all(spectrum, 'gx', 0, 0, tiled=True)  48.2 us
    pallas_call x1, Pallas kernels, interpolate(): pl.pallas_call(sum_kernel, out_shape=jax.ShapeDtypeStruct((2, 4, 16, 128)...  41.1 us
    pallas_call x1, Pallas kernels, turn_weights(): pl.pallas_call(turn_kernel, out_shape=jax.ShapeDtypeStruct((2, 16, 512, 1...  15.6 us
    all_to_all x1, waiting for transfers between devices, local(): got = lax.all_to_all(sent, ('gx', 'gy'), 0, 0, tiled=True)  13.9 us
    pallas_call x1, Pallas kernels, z_transform(): pl.pallas_call(z_kernel, out_shape=jax.ShapeDtypeStruct((8, 2, 16, 32, 12...  9.64 us
    unnamed x25, local copies, waits for them, and re-layouts  9.51 us
  transfers between devices with their start and end apart: 4, of which 2 were waited for; matrix products, arithmetic and copies ran while one was open for 1% of the time, Pallas kernels for 6%

profile of v1, /device:TPU:1, one launch (start us, length us, event | category | flops | bytes accessed | tf_op | source)
XLA Modules:
  0.0 400.4 jit_solution(18415179242680713891)
XLA Ops:
  0.0 0.9 copy-done.7
  1.0 0.9 copy-done.8
  1.9 9.6 %z_transform.1 = f32[8,2,16,32,128]{4,3,2,1,0:T(8,128)S(1)} custom-call(f32[2,2,1024,256]{3,2,1,0:T(8,128)} %bitcast.20, f32[2,2,1024,256]{3,2,1,0:T(8,128)} %bitcast.21, bf16[256,512]{1,0:T(8,128)(2,1)S(1)} %copy-done.7, bf16[256,512]{1,0:T(8,128)(2,1)S(1)} %copy-done.8), custom_call_target="tpu_custom_call" | custom-call | tf_op jit(solution)/shard_map/z_transform/pallas_call | solution.py:86
  11.6 2.0 copy-done
  13.5 6.0 %all-to-all-start.1 = ((f32[8,1024,128]{2,1,0:T(8,128)}), f32[8,1024,128]{2,1,0:T(8,128)}, u32[]{:S(2)}, u32[]{:S(2)}) async-start(f32[8,1024,128]{2,1,0:T(8,128)} %bitcast.15), calls=%async_computation.1 | async-start | bytes 8388608 | tf_op jit(solution)/shard_map/all_to_all | solution.py:265
  19.5 0.7 copy.17
  20.2 48.2 %all-to-all-done.1.data = f32[8,1024,128]{2,1,0:T(8,128)} async-done(((f32[8,1024,128]{2,1,0:T(8,128)}), f32[8,1024,128]{2,1,0:T(8,128)}, u32[]{:S(2)}, u32[]{:S(2)}) %all-to-all-start.1) | async-done | bytes 4194336 | tf_op jit(solution)/shard_map/all_to_all | solution.py:265
  68.4 9.1 %all-to-all-start = ((s32[128,1,4]{2,1,0:T(1,128)}), s32[128,1,4]{2,1,0:T(1,128)S(1)}, u32[]{:S(2)}, u32[]{:S(2)}) async-start(s32[128,1,4]{2,1,0:T(1,128)} %bitcast), calls=%async_computation | async-start | bytes 131072 | tf_op jit(solution)/shard_map/all_to_all | solution.py:255
  77.5 1.6 copy-done.4
  79.1 9.5 %x_transform.1 = f32[16,512,128]{2,1,0:T(8,128)} custom-call(f32[8,1024,128]{2,1,0:T(8,128)} %all-to-all-done.1.data, bf16[1024,1024]{1,0:T(8,128)(2,1)S(1)} %copy-done.3, bf16[1024,1024]{1,0:T(8,128)(2,1)S(1)} %copy-done.4), custom_call_target="tpu_custom_call" | custom-call | tf_op jit(solution)/shard_map/x_transform/pallas_call | solution.py:112
  88.6 7.4 %all-to-all-start.2 = ((f32[16,512,128]{2,1,0:T(8,128)}), f32[16,512,128]{2,1,0:T(8,128)}, u32[]{:S(2)}, u32[]{:S(2)}) async-start(f32[16,512,128]{2,1,0:T(8,128)} %x_transform.1), calls=%async_computation.2 | async-start | bytes 8388608 | tf_op jit(solution)/shard_map/all_to_all | solution.py:267
  96.1 0.5 broadcast.16
  96.6 0.8 reduce.3
  97.8 106.3 %all-gather = s32[128,1,256]{2,1,0:T(1,128)S(1)} all-gather(s32[1,1,256]{2,1,0:T(1,128)S(1)} %bitcast.24), channel_id=1, replica_groups=mesh['gx'=8,'gy'=16] {'gx','gy'}, dimensions={0}, use_global_device_ids=true | all-gather | bytes 132096 | tf_op jit(solution)/shard_map/all_gather | solution.py:258
  204.1 9.4 %y_transform.1 = f32[32,32,8,128]{3,2,1,0:T(8,128)S(1)} custom-call(f32[256,32,128]{2,1,0:T(8,128)} %bitcast.5.data, bf16[256,512]{1,0:T(8,128)(2,1)S(1)} %copy-done.5, bf16[256,512]{1,0:T(8,128)(2,1)S(1)} %copy-done.6), custom_call_target="tpu_custom_call" | custom-call | tf_op jit(solution)/shard_map/y_transform/pallas_call | solution.py:147
  213.5 1.9 copy-done.1
  215.4 105.6 %pick.1 = f32[512,8,128]{2,1,0:T(8,128)S(1)} custom-call(s32[32768]{0:T(1024)S(1)} %bitcast.19, f32[1024,8,128]{2,1,0:T(8,128)} %bitcast.16), custom_call_target="tpu_custom_call" | custom-call | tf_op jit(solution)/shard_map/pick/pallas_call | solution.py:182
  321.0 1.4 copy-done.2
  322.4 6.0 %all-to-all-start.3 = ((f32[128,4,8,128]{3,2,1,0:T(8,128)}), f32[128,4,8,128]{3,2,1,0:T(8,128)S(1)}, u32[]{:S(2)}, u32[]{:S(2)}) async-start(f32[128,4,8,128]{3,2,1,0:T(8,128)} %bitcast.18), calls=%async_computation.3 | async-start | bytes 4194304 | tf_op jit(solution)/shard_map/all_to_all | solution.py:270
  328.4 15.6 %turn_weights.1.weights = f32[2,16,512,128]{3,2,1,0:T(8,128)} custom-call(f32[2,2048,512]{2,1,0:T(8,128)} %bitcast.22), custom_call_target="tpu_custom_call" | custom-call | tf_op jit(solution)/shard_map/turn_weights/pallas_call | solution.py:205
  344.1 13.9 %all-to-all-done.3 = f32[128,4,8,128]{3,2,1,0:T(8,128)S(1)} async-done(((f32[128,4,8,128]{3,2,1,0:T(8,128)}), f32[128,4,8,128]{3,2,1,0:T(8,128)S(1)}, u32[]{:S(2)}, u32[]{:S(2)}) %all-to-all-start.3) | async-done | bytes 2097184 | tf_op jit(solution)/shard_map/all_to_all | solution.py:270
  358.1 41.1 %interpolate.1 = f32[2,4,16,128]{3,2,1,0:T(8,128)S(1)} custom-call(f32[8,2,8,4,8,128]{5,4,3,2,1,0:T(8,128)S(1)} %bitcast.17, f32[2,16,512,128]{3,2,1,0:T(8,128)} %turn_weights.1.weights), custom_call_target="tpu_custom_call" | custom-call | tf_op jit(solution)/shard_map/interpolate/pallas_call | solution.py:239
  399.4 0.3 reduce_sum.19
  399.7 0.6 copy.19
  (27 shorter events, 0.8 us)
Async XLA Ops:
  0.0 0.9 copy-start.7
  1.0 0.9 copy-start.8
  11.6 2.0 copy-start
  13.5 6.0 %copy-start.10 = (s32[1,128,4]{1,2,0:T(4,128)S(1)}, s32[1,128,4]{1,2,0:T(4,128)}, u32[]{:S(2)}) copy-start(s32[1,128,4]{1,2,0:T(4,128)} %param.12) | copy-start | bytes 6148
  13.5 64.0 %copy-start.3 = (bf16[1024,1024]{1,0:T(8,128)(2,1)S(1)}, bf16[1024,1024]{1,0:T(8,128)(2,1)}, u32[]{:S(2)}) copy-start(bf16[1024,1024]{1,0:T(8,128)(2,1)} %constant.18.clone.hi) | copy-start | bytes 6291460
  13.5 54.9 %all-to-all-start.1 = ((f32[8,1024,128]{2,1,0:T(8,128)}), f32[8,1024,128]{2,1,0:T(8,128)}, u32[]{:S(2)}, u32[]{:S(2)}) async-start(f32[8,1024,128]{2,1,0:T(8,128)} %bitcast.15), calls=%async_computation.1 | async-start | bytes 8388608 | tf_op jit(solution)/shard_map/all_to_all | solution.py:265
  68.4 20.2 %all-to-all-start = ((s32[128,1,4]{2,1,0:T(1,128)}), s32[128,1,4]{2,1,0:T(1,128)S(1)}, u32[]{:S(2)}, u32[]{:S(2)}) async-start(s32[128,1,4]{2,1,0:T(1,128)} %bitcast), calls=%async_computation | async-start | bytes 131072 | tf_op jit(solution)/shard_map/all_to_all | solution.py:255
  77.5 1.6 copy-start.4
  88.6 7.4 %copy-start.9 = (s32[16,16]{1,0:T(8,128)S(1)}, s32[16,16]{1,0:T(8,128)}, u32[]{:S(2)}) copy-start(s32[16,16]{1,0:T(8,128)} %param.13) | copy-start | bytes 3076
  88.6 115.4 %copy-start.5 = (bf16[256,512]{1,0:T(8,128)(2,1)S(1)}, bf16[256,512]{1,0:T(8,128)(2,1)}, u32[]{:S(2)}) copy-start(bf16[256,512]{1,0:T(8,128)(2,1)} %constant.20.clone.hi) | copy-start | bytes 786436
  88.6 115.4 %copy-start.6 = (bf16[256,512]{1,0:T(8,128)(2,1)S(1)}, bf16[256,512]{1,0:T(8,128)(2,1)}, u32[]{:S(2)}) copy-start(bf16[256,512]{1,0:T(8,128)(2,1)} %constant.21.clone.lo) | copy-start | bytes 786436
  88.6 115.4 %all-to-all-start.2 = ((f32[16,512,128]{2,1,0:T(8,128)}), f32[16,512,128]{2,1,0:T(8,128)}, u32[]{:S(2)}, u32[]{:S(2)}) async-start(f32[16,512,128]{2,1,0:T(8,128)} %x_transform.1), calls=%async_computation.2 | async-start | bytes 8388608 | tf_op jit(solution)/shard_map/all_to_all | solution.py:267
  213.5 2.0 copy-start.1
  321.0 1.4 copy-start.2
  322.4 35.7 %all-to-all-start.3 = ((f32[128,4,8,128]{3,2,1,0:T(8,128)}), f32[128,4,8,128]{3,2,1,0:T(8,128)S(1)}, u32[]{:S(2)}, u32[]{:S(2)}) async-start(f32[128,4,8,128]{3,2,1,0:T(8,128)} %bitcast.18), calls=%async_computation.3 | async-start | bytes 4194304 | tf_op jit(solution)/shard_map/all_to_all | solution.py:270
  328.4 15.6 %copy-start.11 = (s32[16]{0:T(128)S(1)}, s32[16]{0:T(128)}, u32[]{:S(2)}) copy-start(s32[16]{0:T(128)} %param.15) | copy-start | bytes 196

commit v2 on v1

--- a/solution.py
+++ b/solution.py
@@ -45,7 +45,12 @@
 
 def y_table():
     phase = angle(np.arange(NY), np.arange(NY), NY)
-    return split_table(np.concatenate([np.cos(phase), np.sin(phase)], 1))
+    cos, sin = np.cos(phase), np.sin(phase)
+    whole = np.zeros((2, NY, 2, NY))
+    whole[0, :, 0], whole[1, :, 0] = cos, sin
+    whole[0, :, 1], whole[1, :, 1] = -sin, cos
+    whole = whole.reshape(2, NY, 2, 32, 8).transpose(0, 1, 3, 2, 4)
+    return split_table(whole.reshape(512, 512))
 
 
 def halves(value):
@@ -120,82 +125,85 @@
     )(data, jnp.asarray(hi), jnp.asarray(lo))
 
 
-def y_kernel(data, hi, lo, out):
+def y_group(g, data, hi, lo, table):
     flat = data.reshape(2048, 128)
-    sign = jnp.where(lax.broadcasted_iota(jnp.int32, (256, 128), 1) < 64, 1.0, -1.0)
-
-    def pair(p, carry):
-        rows, swapped = [], []
-        for k in range(2):
-            part = flat[pl.ds(2 * p + k, 256, stride=8), :]
-            rows.append(part)
-            swapped.append(pltpu.roll(part, 64, 1) * sign)
-        both = jnp.concatenate(
-            [jnp.concatenate(rows, 1), jnp.concatenate(swapped, 1)], 0
-        )
-        res = dot3((hi[...], lo[...]), halves(both), ((1,), (0,)))
-        for k in range(2):
-            out[:, 2 * p + k] = res[:, k * 128 : (k + 1) * 128].reshape(32, 8, 128)
-        return carry
-
-    lax.fori_loop(0, 4, pair, 0)
-
-
-def y_transform(data):
+    lane = lax.broadcasted_iota(jnp.int32, (64, 128), 1)
+
+    def four(p, carry):
+        rows = []
+        for k in range(4):
+            turned = flat[pl.ds(4 * p + k, 256, stride=8), :].T
+            rows.append(jnp.concatenate([turned[:64], turned[64:]], 1))
+        res = dot3(halves(jnp.concatenate(rows, 0)), (hi[...], lo[...]), ((1,), (0,)))
+        for k in range(4):
+            bz = 8 * g + 4 * p + k
+            for high in range(4):
+                part = res[k * 64 : (k + 1) * 64, high * 128 : (high + 1) * 128]
+                for low in range(8):
+                    source = low * 16 + jnp.bitwise_and(lane, 15)
+                    at = pl.multiple_of((bz * 32 + high * 8 + low) * 64, 64)
+                    table[pl.ds(at, 64), :] = jnp.take_along_axis(part, source, axis=1)
+        return carry
+
+    lax.fori_loop(0, 2, four, 0)
+
+
+def pick_group(rows, table, raw, out):
+    def eight(t, carry):
+        for s in range(8):
+            for g in range(8):
+                lanes = slice(g * 16, g * 16 + 16)
+                row = rows[g * 256 + t * 8 + s]
+                raw[pl.ds(t * 8 + s, 1), lanes] = table[pl.ds(row, 1), lanes]
+        return carry
+
+    lax.fori_loop(0, 32, eight, 0)
+    for h in range(2):
+        turned = raw[h * 128 : (h + 1) * 128, :].T
+        for g in range(8):
+            out[g, h] = turned[g * 16 : (g + 1) * 16]
+
+
+def pick_kernel(data, rows, hi, lo, out, table, raw):
+    g = pl.program_id(0)
+
+    @pl.when(g < 4)
+    def _():
+        y_group(g, data, hi, lo, table)
+
+    @pl.when(g >= 4)
+    def _():
+        pick_group(rows, table, raw, out)
+
+
+def y_pick(data, rows):
     hi, lo = y_table()
-    whole = pl.BlockSpec((256, 512), lambda g: (0, 0))
-    return pl.pallas_call(
-        y_kernel,
-        out_shape=jax.ShapeDtypeStruct((32, 32, 8, 128), F32),
-        grid=(4,),
-        in_specs=[pl.BlockSpec((256, 8, 128), lambda g: (0, g, 0)), whole, whole],
-        out_specs=pl.BlockSpec((32, 8, 8, 128), lambda g: (0, g, 0, 0)),
-        compiler_params=pltpu.CompilerParams(vmem_limit_bytes=VMEM_LIMIT),
-        name="y_transform",
-    )(data.reshape(256, 32, 128), jnp.asarray(hi), jnp.asarray(lo))
-
-
-def pick_kernel(ids, table, out):
-    lane = jnp.bitwise_and(lax.broadcasted_iota(jnp.int32, (8, 128), 1), 63)
-
-    def group(t, carry):
-        chains = [None] * 4
-        for i in range(64):
-            block = ids[t * 64 + i]
-            tile = table[jnp.bitwise_and(block, 1023)]
-            shift = jnp.bitwise_and(i - jnp.right_shift(block, 10), 127)
-            moved = pltpu.roll(tile, shift, 1)
-            old = chains[i % 4]
-            chains[i % 4] = moved if old is None else jnp.where(lane == i, moved, old)
-        low = jnp.bitwise_and(lane, 3)
-        out[t] = jnp.where(
-            low < 2,
-            jnp.where(low == 0, chains[0], chains[1]),
-            jnp.where(low == 2, chains[2], chains[3]),
-        )
-        return carry
-
-    lax.fori_loop(0, 32, group, 0)
-
-
-def pick(ids, table):
+    whole = pl.BlockSpec((512, 512), lambda g: (0, 0))
+    late = lambda g: jnp.maximum(g - 4, 0)
     return pl.pallas_call(
         pick_kernel,
-        out_shape=jax.ShapeDtypeStruct((512, 8, 128), F32),
-        grid=(16,),
+        out_shape=jax.ShapeDtypeStruct((128, 2, 16, 128), F32),
+        grid=(20,),
         in_specs=[
-            pl.BlockSpec((2048,), lambda g: (g,), memory_space=pltpu.SMEM),
-            pl.BlockSpec((1024, 8, 128), lambda g: (0, 0, 0)),
+            pl.BlockSpec((256, 8, 128), lambda g: (0, jnp.minimum(g, 3), 0)),
+            pl.BlockSpec((2048,), lambda g: (late(g),), memory_space=pltpu.SMEM),
+            whole,
+            whole,
         ],
-        out_specs=pl.BlockSpec((32, 8, 128), lambda g: (g, 0, 0)),
-        compiler_params=pltpu.CompilerParams(vmem_limit_bytes=VMEM_LIMIT),
-        name="pick",
-    )(ids, table.reshape(1024, 8, 128))
+        out_specs=pl.BlockSpec((8, 2, 16, 128), lambda g: (late(g), 0, 0, 0)),
+        scratch_shapes=[pltpu.VMEM((65536, 128), F32), pltpu.VMEM((256, 128), F32)],
+        compiler_params=pltpu.CompilerParams(vmem_limit_bytes=VMEM_LIMIT),
+        name="y_pick",
+    )(data.reshape(256, 32, 128), rows, jnp.asarray(hi), jnp.asarray(lo))
 
 
 def turn_kernel(weights, out):
     def one(n, carry):
-        out[0, n] = weights[0, pl.ds(n, 128, stride=16), :].T
+        turned = weights[0, pl.ds(n, 128, stride=16), :].T
+        for u in range(2):
+            for v in range(8):
+                at = (u * 8 + v) * 8
+                out[0, n, pl.ds(u * 64 + v, 8, stride=8), :] = turned[at : at + 8]
         return carry
 
     lax.fori_loop(0, 16, one, 0)
@@ -214,23 +222,18 @@
 
 
 def sum_kernel(got, weights, out):
-    low = lax.broadcasted_iota(jnp.int32, (8, 128), 1) < 64
-
-    def one(t, carry):
-        w, u = t // 8, t % 8
-        values = []
-        for c in range(2):
-            first, second = got[w, c, u, 0], got[w, c, u, 1]
-            values.append(jnp.where(low, first, pltpu.roll(second, 64, 1)))
-            values.append(jnp.where(low, pltpu.roll(first, 64, 1), second))
+    def one(u, carry):
         sums = list(carry)
-        for n in range(4):
-            factor = weights[0, n, pl.ds(u * 64 + w, 8, stride=8), :]
+        for w in range(8):
+            at = pl.multiple_of(u * 64 + w * 8, 8)
+            factors = [weights[0, n, pl.ds(at, 8), :] for n in range(4)]
             for k in range(4):
-                sums[n * 4 + k] = sums[n * 4 + k] + factor * values[k]
+                value = got[w, k // 2, u, 0, k % 2]
+                for n in range(4):
+                    sums[n * 4 + k] = sums[n * 4 + k] + factors[n] * value
         return tuple(sums)
 
-    sums = lax.fori_loop(0, 64, one, (jnp.zeros((8, 128), F32),) * 16)
+    sums = lax.fori_loop(0, 8, one, (jnp.zeros((8, 128), F32),) * 16)
     rows = [jnp.sum(s, 0, keepdims=True) for s in sums]
     out[0, 0] = jnp.concatenate(rows, 0)
 
@@ -241,7 +244,7 @@
         out_shape=jax.ShapeDtypeStruct((2, 4, 16, 128), F32),
         grid=(2, 4),
         in_specs=[
-            pl.BlockSpec((8, 2, 8, 2, 8, 128), lambda h, n: (0, 0, 0, h, 0, 0)),
+            pl.BlockSpec((8, 2, 8, 1, 2, 8, 128), lambda h, n: (0, 0, 0, h, 0, 0, 0)),
             pl.BlockSpec((1, 4, 512, 128), lambda h, n: (h, n, 0, 0)),
         ],
         out_specs=pl.BlockSpec((1, 1, 16, 128), lambda h, n: (h, n, 0, 0)),
@@ -250,25 +253,26 @@
     )(got, weights)
 
 
-def block_ids(send_lists, seg_slots):
+def table_rows(send_lists, seg_slots):
     both = ("gx", "gy")
     lists = lax.all_to_all(send_lists[0], both, 0, 0, tiled=True).reshape(1, 512)
     hit = seg_slots.reshape(256, 1) == jnp.arange(512, dtype=jnp.int32)[None, :]
     ids = jnp.sum(jnp.where(hit, lists, 0), 1)
-    return lax.all_gather(ids, both, axis=0, tiled=True)
+    rows = (ids & 31) * 2048 + ((ids >> 5) & 31) * 64 + (ids >> 10)
+    sent = jnp.broadcast_to(rows[None, :], (DEVS, 256))
+    return lax.all_to_all(sent, both, 0, 0, tiled=True).reshape(-1)
 
 
 def local(coil_images, send_lists, seg_slots, weights, counts):
-    ids = block_ids(send_lists, seg_slots)
+    rows = table_rows(send_lists, seg_slots)
     turned = turn_weights(weights)
     spectrum = z_transform(coil_images).reshape(8, 1024, 128)
     spectrum = lax.all_to_all(spectrum, "gx", 0, 0, tiled=True)
     spectrum = x_transform(spectrum)
     spectrum = lax.all_to_all(spectrum, "gy", 0, 0, tiled=True)
-    table = y_transform(spectrum)
-    sent = pick(ids, table).reshape(128, 4, 8, 128)
+    sent = y_pick(spectrum, rows)
     got = lax.all_to_all(sent, ("gx", "gy"), 0, 0, tiled=True)
-    sums = interpolate(got.reshape(8, 2, 8, 4, 8, 128), turned)
+    sums = interpolate(got.reshape(8, 2, 8, 2, 2, 8, 128), turned)
     sums = sums.reshape(2, 16, 2, 2, 8, 16).sum(-1)
     samples = sums.transpose(0, 4, 2, 3, 1).reshape(16, 2, 2, 16)
     live = jnp.arange(16, dtype=jnp.int32) < counts[:, None, None, None]

time: 401 us -> 257 us (0.64)
  Pallas kernels: 191 us -> 93.5 us
  blocking collectives: 106 us -> 57.1 us
    all_gather x1 -> x0, blocking collectives: 106 us -> none  [block_ids(): return lax.all_gather(ids, both, axis=0, tiled=True)]
    pallas_call x2 -> x1, Pallas kernels: 115 us -> 51.7 us  [y_pick(): pl.pallas_call(pick_kernel, out_shape=jax.ShapeDtypeStruct((128, 2, 16, 1...]
    all_to_all x0 -> x1, blocking collectives: none -> 57.1 us  [local(): spectrum = lax.all_to_all(spectrum, 'gy', 0, 0, tiled=True)]
    pallas_call x1, Pallas kernels: 41.1 us -> 6.99 us  [interpolate(): pl.pallas_call(sum_kernel, out_shape=jax.ShapeDtypeStruct((2, 4, 16, 128)...]
    unnamed x25 -> x21, local copies, waits for them, and re-layouts: 9.51 us -> 8.23 us
  transfers between devices with their start and end apart: 4 -> 4, of which waited for: 2 -> 2; matrix products, arithmetic and copies ran while one was open for 1% -> 1% of each run, Pallas kernels for 6% -> 14%
where the time goes in v2:
time: 257 us; the launch traced here: 256 us
  Pallas kernels  93.5 us (36%)
  waiting for transfers between devices  61 us (24%)
  blocking collectives  57.1 us (22%)
  starting transfers between devices  32.3 us (13%)
  local copies, waits for them, and re-layouts  10.6 us (4%)
    all_to_all x1, blocking collectives, local(): spectrum = lax.all_to_all(spectrum, 'gy', 0, 0, tiled=True)  57.1 us
    pallas_call x1, Pallas kernels, y_pick(): pl.pallas_call(pick_kernel, out_shape=jax.ShapeDtypeStruct((128, 2, 16, 1...  51.7 us
    all_to_all x1, waiting for transfers between devices, local(): spectrum = lax.all_to_all(spectrum, 'gx', 0, 0, tiled=True)  47.2 us
    pallas_call x1, Pallas kernels, turn_weights(): pl.pallas_call(turn_kernel, out_shape=jax.ShapeDtypeStruct((2, 16, 512, 1...  15.6 us
    all_to_all x1, waiting for transfers between devices, local(): got = lax.all_to_all(sent, ('gx', 'gy'), 0, 0, tiled=True)  13.8 us
    all_to_all x1, starting transfers between devices, table_rows(): lax.all_to_all(send_lists[0], both, 0, 0, tiled=True).reshape(1, 512)  11.5 us
    pallas_call x1, Pallas kernels, z_transform(): pl.pallas_call(z_kernel, out_shape=jax.ShapeDtypeStruct((8, 2, 16, 32, 12...  9.64 us
    pallas_call x1, Pallas kernels, x_transform(): pl.pallas_call(x_kernel, out_shape=jax.ShapeDtypeStruct((16, 512, 128), F...  9.48 us
  transfers between devices with their start and end apart: 4, of which 2 were waited for; matrix products, arithmetic and copies ran while one was open for 1% of the time, Pallas kernels for 14%

profile of v2, /device:TPU:1, one launch (start us, length us, event | category | flops | bytes accessed | tf_op | source)
XLA Modules:
  0.0 256.0 jit_solution(9993432925887723650)
XLA Ops:
  0.0 1.4 copy.17
  1.4 11.5 %all-to-all-start.2 = ((s32[128,1,4]{2,1,0:T(1,128)}), s32[128,1,4]{2,1,0:T(1,128)S(1)}, u32[]{:S(2)}, u32[]{:S(2)}) async-start(s32[128,1,4]{2,1,0:T(1,128)} %bitcast.3), calls=%async_computation.2 | async-start | bytes 131072 | tf_op jit(solution)/shard_map/all_to_all | solution.py:258
  12.9 0.9 copy-done.6
  13.9 0.9 copy-done.7
  14.8 9.6 %z_transform.1 = f32[8,2,16,32,128]{4,3,2,1,0:T(8,128)S(1)} custom-call(f32[2,2,1024,256]{3,2,1,0:T(8,128)} %bitcast.15, f32[2,2,1024,256]{3,2,1,0:T(8,128)} %bitcast.16, bf16[256,512]{1,0:T(8,128)(2,1)S(1)} %copy-done.6, bf16[256,512]{1,0:T(8,128)(2,1)S(1)} %copy-done.7), custom_call_target="tpu_custom_call" | custom-call | tf_op jit(solution)/shard_map/z_transform/pallas_call | solution.py:91
  24.5 2.0 copy-done
  26.4 5.6 %all-to-all-start = ((f32[8,1024,128]{2,1,0:T(8,128)}), f32[8,1024,128]{2,1,0:T(8,128)}, u32[]{:S(2)}, u32[]{:S(2)}) async-start(f32[8,1024,128]{2,1,0:T(8,128)} %bitcast.12), calls=%async_computation | async-start | bytes 8388608 | tf_op jit(solution)/shard_map/all_to_all | solution.py:270
  32.2 0.5 broadcast.49
  32.7 0.8 reduce.3
  33.6 0.2 select_reduce_fusion
  33.8 47.2 %all-to-all-done.data = f32[8,1024,128]{2,1,0:T(8,128)} async-done(((f32[8,1024,128]{2,1,0:T(8,128)}), f32[8,1024,128]{2,1,0:T(8,128)}, u32[]{:S(2)}, u32[]{:S(2)}) %all-to-all-start) | async-done | bytes 4194336 | tf_op jit(solution)/shard_map/all_to_all | solution.py:270
  81.0 0.7 broadcast_in_dim.39
  81.7 7.7 %all-to-all-start.3 = ((s32[128,1,256]{2,1,0:T(1,128)}), s32[128,1,256]{2,1,0:T(1,128)S(1)}, u32[]{:S(2)}, u32[]{:S(2)}) async-start(s32[128,1,256]{2,1,0:T(1,128)} %broadcast_in_dim.39), calls=%async_computation.3 | async-start | bytes 262144 | tf_op jit(solution)/shard_map/all_to_all | solution.py:263
  89.5 1.6 copy-done.3
  91.1 9.5 %x_transform.1 = f32[16,512,128]{2,1,0:T(8,128)} custom-call(f32[8,1024,128]{2,1,0:T(8,128)} %all-to-all-done.data, bf16[1024,1024]{1,0:T(8,128)(2,1)S(1)} %copy-done.2, bf16[1024,1024]{1,0:T(8,128)(2,1)S(1)} %copy-done.3), custom_call_target="tpu_custom_call" | custom-call | tf_op jit(solution)/shard_map/x_transform/pallas_call | solution.py:117
  100.6 57.1 %all_to_all.30 = f32[16,512,128]{2,1,0:T(8,128)} all-to-all(f32[16,512,128]{2,1,0:T(8,128)} %x_transform.1), channel_id=1, replica_groups=mesh['gx'=8,'gy'=16] {'gy'}, dimensions={0} | all-to-all | bytes 8388608 | tf_op jit(solution)/shard_map/all_to_all | solution.py:272
  157.7 51.7 %y_pick.1 = f32[128,2,16,128]{3,2,1,0:T(8,128)S(1)} custom-call(f32[256,32,128]{2,1,0:T(8,128)} %bitcast.17, s32[32768]{0:T(1024)S(1)} %bitcast.14, bf16[512,512]{1,0:T(8,128)(2,1)S(1)} %copy-done.4, bf16[512,512]{1,0:T(8,128)(2,1)S(1)} %copy-done.5), custom_call_target="tpu_custom_call" | custom-call | tf_op jit(solution)/shard_map/y_pick/pallas_call | solution.py:183
  209.5 1.4 copy-done.1
  210.8 7.5 %all-to-all-start.4 = ((f32[128,2,16,128]{3,2,1,0:T(8,128)}), f32[128,2,16,128]{3,2,1,0:T(8,128)S(1)}, u32[]{:S(2)}, u32[]{:S(2)}) async-start(f32[128,2,16,128]{3,2,1,0:T(8,128)} %copy-done.1), calls=%async_computation.4 | async-start | bytes 4194304 | tf_op jit(solution)/shard_map/all_to_all | solution.py:274
  218.3 15.6 %turn_weights.1.weights = f32[2,16,512,128]{3,2,1,0:T(8,128)} custom-call(f32[2,2048,512]{2,1,0:T(8,128)} %bitcast.18), custom_call_target="tpu_custom_call" | custom-call | tf_op jit(solution)/shard_map/turn_weights/pallas_call | solution.py:213
  234.0 13.8 %all-to-all-done.4 = f32[128,2,16,128]{3,2,1,0:T(8,128)S(1)} async-done(((f32[128,2,16,128]{3,2,1,0:T(8,128)}), f32[128,2,16,128]{3,2,1,0:T(8,128)S(1)}, u32[]{:S(2)}, u32[]{:S(2)}) %all-to-all-start.4) | async-done | bytes 2097184 | tf_op jit(solution)/shard_map/all_to_all | solution.py:274
  247.8 7.0 %interpolate.1 = f32[2,4,16,128]{3,2,1,0:T(8,128)S(1)} custom-call(f32[8,2,8,2,2,8,128]{6,5,4,3,2,1,0:T(8,128)S(1)} %bitcast.13, f32[2,16,512,128]{3,2,1,0:T(8,128)} %turn_weights.1.weights), custom_call_target="tpu_custom_call" | custom-call | tf_op jit(solution)/shard_map/interpolate/pallas_call | solution.py:242
  255.0 0.3 reduce_sum.19
  255.3 0.6 copy.19
  (24 shorter events, 0.6 us)
Async XLA Ops:
  1.4 25.0 %all-to-all-start.2 = ((s32[128,1,4]{2,1,0:T(1,128)}), s32[128,1,4]{2,1,0:T(1,128)S(1)}, u32[]{:S(2)}, u32[]{:S(2)}) async-start(s32[128,1,4]{2,1,0:T(1,128)} %bitcast.3), calls=%async_computation.2 | async-start | bytes 131072 | tf_op jit(solution)/shard_map/all_to_all | solution.py:258
  12.9 1.0 copy-start.6
  13.9 0.9 copy-start.7
  24.5 2.0 copy-start
  26.4 5.6 %copy-start.8 = (s32[16,16]{1,0:T(8,128)S(1)}, s32[16,16]{1,0:T(8,128)}, u32[]{:S(2)}) copy-start(s32[16,16]{1,0:T(8,128)} %param.13) | copy-start | bytes 3076
  26.4 63.0 %copy-start.2 = (bf16[1024,1024]{1,0:T(8,128)(2,1)S(1)}, bf16[1024,1024]{1,0:T(8,128)(2,1)}, u32[]{:S(2)}) copy-start(bf16[1024,1024]{1,0:T(8,128)(2,1)} %constant.28.clone.hi) | copy-start | bytes 6291460
  26.4 54.6 %all-to-all-start = ((f32[8,1024,128]{2,1,0:T(8,128)}), f32[8,1024,128]{2,1,0:T(8,128)}, u32[]{:S(2)}, u32[]{:S(2)}) async-start(f32[8,1024,128]{2,1,0:T(8,128)} %bitcast.12), calls=%async_computation | async-start | bytes 8388608 | tf_op jit(solution)/shard_map/all_to_all | solution.py:270
  81.7 18.8 %all-to-all-start.3 = ((s32[128,1,256]{2,1,0:T(1,128)}), s32[128,1,256]{2,1,0:T(1,128)S(1)}, u32[]{:S(2)}, u32[]{:S(2)}) async-start(s32[128,1,256]{2,1,0:T(1,128)} %broadcast_in_dim.39), calls=%async_computation.3 | async-start | bytes 262144 | tf_op jit(solution)/shard_map/all_to_all | solution.py:263
  89.5 1.6 copy-start.3
  100.5 57.1 %copy-start.4 = (bf16[512,512]{1,0:T(8,128)(2,1)S(1)}, bf16[512,512]{1,0:T(8,128)(2,1)}, u32[]{:S(2)}) copy-start(bf16[512,512]{1,0:T(8,128)(2,1)} %constant.30.clone.hi) | copy-start | bytes 1572868
  100.6 57.1 %copy-start.5 = (bf16[512,512]{1,0:T(8,128)(2,1)S(1)}, bf16[512,512]{1,0:T(8,128)(2,1)}, u32[]{:S(2)}) copy-start(bf16[512,512]{1,0:T(8,128)(2,1)} %constant.31.clone.lo) | copy-start | bytes 1572868
  209.4 1.4 copy-start.1
  210.8 37.0 %all-to-all-start.4 = ((f32[128,2,16,128]{3,2,1,0:T(8,128)}), f32[128,2,16,128]{3,2,1,0:T(8,128)S(1)}, u32[]{:S(2)}, u32[]{:S(2)}) async-start(f32[128,2,16,128]{3,2,1,0:T(8,128)} %copy-done.1), calls=%async_computation.4 | async-start | bytes 4194304 | tf_op jit(solution)/shard_map/all_to_all | solution.py:274
  218.3 15.6 %copy-start.9 = (s32[16]{0:T(128)S(1)}, s32[16]{0:T(128)}, u32[]{:S(2)}) copy-start(s32[16]{0:T(128)} %param.15) | copy-start | bytes 196

commit v3 on v2

--- a/solution.py
+++ b/solution.py
@@ -27,7 +27,8 @@
 
 
 def z_table():
-    order = (np.arange(8)[:, None] + 8 * np.arange(32)[None, :]).reshape(-1)
+    bz = np.arange(32).reshape(4, 1, 8)
+    order = (np.arange(8)[None, :, None] + 8 * bz).reshape(-1)
     phase = angle(order, np.arange(NZ), NZ)
     scale = 1.0 / math.sqrt(NX * NY * NZ)
     return split_table(np.concatenate([np.cos(phase), np.sin(phase)], 1) * scale)
@@ -65,74 +66,170 @@
     return one(left[0], right[0]) + (one(left[0], right[1]) + one(left[1], right[0]))
 
 
-def z_kernel(near, far, hi, lo, out):
-    def pair(yp, carry):
-        rows, swapped = [], []
-        for k in range(2):
-            at = pl.ds(2 * yp + k, 64, stride=16)
-            re, im = (jnp.concatenate([near[0, q, at, :], far[0, q, at, :]], 1) for q in range(2))
-            rows += [re, im]
-            swapped += [im, -re]
-        data = jnp.concatenate(
-            [jnp.concatenate(rows, 0), jnp.concatenate(swapped, 0)], 1
-        )
-        res = dot3((hi[...], lo[...]), halves(data), ((1,), (1,)))
-        for k in range(2):
-            out[:, 0, 2 * yp + k] = res[:, k * 128 : (k + 1) * 128].reshape(8, 32, 128)
-        return carry
-
-    lax.fori_loop(0, 8, pair, 0)
-
-
-def z_transform(images):
-    images = images.reshape(2, 2, 1024, 256)
-    hi, lo = z_table()
-    whole = pl.BlockSpec((256, 512), lambda c: (0, 0))
+def z_pair(yp, c, image, hi, lo, sent):
+    rows, swapped = [], []
+    for k in range(2):
+        at = pl.ds(2 * yp + k, 64, stride=16)
+        re, im = (
+            jnp.concatenate([image[half, c, q, at, :] for half in range(2)], 1)
+            for q in range(2)
+        )
+        rows += [re, im]
+        swapped += [im, -re]
+    data = jnp.concatenate([jnp.concatenate(rows, 0), jnp.concatenate(swapped, 0)], 1)
+    res = dot3((hi[...], lo[...]), halves(data), ((1,), (1,)))
+    for k in range(2):
+        part = res[:, k * 128 : (k + 1) * 128].reshape(4, 8, 8, 128)
+        sent[:, :, c, 2 * yp + k] = part
+
+
+def grid_kernel(
+    images, z_hi_in, z_lo_in, x_hi_in, x_lo_in, out,
+    image, z_hi, z_lo, x_hi, x_lo, z_out, x_in, x_out,
+    load_sem, self_sem, send1, recv1, send2, recv2,
+):
+    gx, gy = lax.axis_index("gx"), lax.axis_index("gy")
+    loads = [
+        pltpu.make_async_copy(src, dst, load_sem.at[i])
+        for i, (src, dst) in enumerate(
+            [(z_hi_in, z_hi), (z_lo_in, z_lo)]
+            + [
+                (images.at[c, q, :, pl.ds(half * 128, 128)], image.at[half, c, q])
+                for c in range(2)
+                for q in range(2)
+                for half in range(2)
+            ]
+            + [(x_hi_in, x_hi), (x_lo_in, x_lo)]
+        )
+    ]
+    for load in loads:
+        load.start()
+
+    barrier = pltpu.get_barrier_semaphore()
+    for r in range(1, GX):
+        pl.semaphore_signal(barrier, inc=1, device_id={"gx": (gx + r) % GX})
+    for r in range(1, GY):
+        pl.semaphore_signal(barrier, inc=1, device_id={"gy": (gy + r) % GY})
+    pl.semaphore_wait(barrier, GX + GY - 2)
+
+    def over_x(k, r):
+        to = (gx + r) % GX
+        return pltpu.make_async_remote_copy(
+            src_ref=z_out.at[k, to],
+            dst_ref=x_in.at[k, gx],
+            send_sem=send1.at[k, r],
+            recv_sem=recv1.at[k, r],
+            device_id={"gx": to},
+        )
+
+    def over_y(k, r):
+        to = (gy + r) % GY
+        return pltpu.make_async_remote_copy(
+            src_ref=x_out.at[k, to],
+            dst_ref=out.at[k, gy],
+            send_sem=send2.at[k, r],
+            recv_sem=recv2.at[k, r],
+            device_id={"gy": to},
+        )
+
+    def own_x(k):
+        return pltpu.make_async_copy(z_out.at[k, gx], x_in.at[k, gx], self_sem.at[0, k])
+
+    def own_y(k):
+        return pltpu.make_async_copy(x_out.at[k, gy], out.at[k, gy], self_sem.at[1, k])
+
+    for load in loads[:2]:
+        load.wait()
+    for c in range(2):
+        for load in loads[2 + 4 * c : 6 + 4 * c]:
+            load.wait()
+
+        def pair(yp, carry):
+            z_pair(yp, c, image, z_hi, z_lo, z_out)
+            return carry
+
+        lax.fori_loop(0, 8, pair, 0)
+    for load in loads[10:]:
+        load.wait()
+
+    def send_x(k, carry):
+        for r in range(1, GX):
+            over_x(k, r).start()
+        own_x(k).start()
+        return carry
+
+    lax.fori_loop(0, 4, send_x, 0)
+
+    def chunk(k, carry):
+        own_x(k).wait()
+        for r in range(1, GX):
+            over_x(k, r).wait_recv()
+        rows = jnp.concatenate(
+            [x_in[k, a].reshape(256, 128) for a in range(8)], 1
+        )
+        res = dot3(halves(rows), (x_hi[...], x_lo[...]), ((1,), (0,)))
+        for c in range(2):
+            for u in range(8):
+                x_out[k, c * 8 + u] = res[
+                    c * 128 : (c + 1) * 128, u * 128 : (u + 1) * 128
+                ].reshape(16, 8, 128)
+        for r in range(1, GY):
+            over_y(k, r).start()
+        own_y(k).start()
+        return carry
+
+    lax.fori_loop(0, 4, chunk, 0)
+
+    def finish(k, carry):
+        own_y(k).wait()
+        for r in range(1, GX):
+            over_x(k, r).wait_send()
+        for r in range(1, GY):
+            over_y(k, r).wait()
+        return carry
+
+    lax.fori_loop(0, 4, finish, 0)
+
+
+def grid_values(images):
+    tables = [jnp.asarray(t) for t in z_table() + x_table()]
+    anywhere = pl.BlockSpec(memory_space=pl.ANY)
+    sems = pltpu.SemaphoreType.DMA
     return pl.pallas_call(
-        z_kernel,
-        out_shape=jax.ShapeDtypeStruct((8, 2, 16, 32, 128), F32),
-        grid=(2,),
-        in_specs=[
-            pl.BlockSpec((1, 2, 1024, 128), lambda c: (c, 0, 0, 0)),
-            pl.BlockSpec((1, 2, 1024, 128), lambda c: (c, 0, 0, 1)),
-            whole,
-            whole,
+        grid_kernel,
+        out_shape=jax.ShapeDtypeStruct((4, 16, 16, 8, 128), F32),
+        in_specs=[anywhere] * 5,
+        out_specs=anywhere,
+        scratch_shapes=[
+            pltpu.VMEM((2, 2, 2, 1024, 128), F32),
+            pltpu.VMEM((256, 512), BF16),
+            pltpu.VMEM((256, 512), BF16),
+            pltpu.VMEM((1024, 1024), BF16),
+            pltpu.VMEM((1024, 1024), BF16),
+            pltpu.VMEM((4, 8, 2, 16, 8, 128), F32),
+            pltpu.VMEM((4, 8, 2, 16, 8, 128), F32),
+            pltpu.VMEM((4, 16, 16, 8, 128), F32),
+            sems((12,)),
+            sems((2, 4)),
+            sems((4, GX)),
+            sems((4, GX)),
+            sems((4, GY)),
+            sems((4, GY)),
         ],
-        out_specs=pl.BlockSpec((8, 1, 16, 32, 128), lambda c: (0, c, 0, 0, 0)),
-        compiler_params=pltpu.CompilerParams(vmem_limit_bytes=VMEM_LIMIT),
-        name="z_transform",
-    )(images, images, jnp.asarray(hi), jnp.asarray(lo))
-
-
-def x_kernel(data, hi, lo, out):
-    rows = jnp.concatenate([data[a] for a in range(8)], 1)
-    res = dot3(halves(rows), (hi[...], lo[...]), ((1,), (0,)))
-    for u in range(8):
-        out[u] = res[:, u * 128 : (u + 1) * 128]
-
-
-def x_transform(data):
-    hi, lo = x_table()
-    whole = pl.BlockSpec((1024, 1024), lambda r: (0, 0))
-    return pl.pallas_call(
-        x_kernel,
-        out_shape=jax.ShapeDtypeStruct((16, 512, 128), F32),
-        grid=(4,),
-        in_specs=[pl.BlockSpec((8, 256, 128), lambda r: (0, r, 0)), whole, whole],
-        out_specs=pl.BlockSpec((8, 256, 128), lambda r: (r // 2, r % 2, 0)),
-        compiler_params=pltpu.CompilerParams(vmem_limit_bytes=VMEM_LIMIT),
-        name="x_transform",
-    )(data, jnp.asarray(hi), jnp.asarray(lo))
+        compiler_params=pltpu.CompilerParams(
+            vmem_limit_bytes=VMEM_LIMIT, collective_id=0, has_side_effects=True
+        ),
+        name="grid_values",
+    )(images.reshape(2, 2, 1024, 256), *tables)
 
 
 def y_group(g, data, hi, lo, table):
-    flat = data.reshape(2048, 128)
     lane = lax.broadcasted_iota(jnp.int32, (64, 128), 1)
 
     def four(p, carry):
         rows = []
         for k in range(4):
-            turned = flat[pl.ds(4 * p + k, 256, stride=8), :].T
+            turned = data[pl.ds(4 * p + k, 256, stride=8), :].T
             rows.append(jnp.concatenate([turned[:64], turned[64:]], 1))
         res = dot3(halves(jnp.concatenate(rows, 0)), (hi[...], lo[...]), ((1,), (0,)))
         for k in range(4):
@@ -185,7 +282,7 @@
         out_shape=jax.ShapeDtypeStruct((128, 2, 16, 128), F32),
         grid=(20,),
         in_specs=[
-            pl.BlockSpec((256, 8, 128), lambda g: (0, jnp.minimum(g, 3), 0)),
+            pl.BlockSpec((2048, 128), lambda g: (jnp.minimum(g, 3), 0)),
             pl.BlockSpec((2048,), lambda g: (late(g),), memory_space=pltpu.SMEM),
             whole,
             whole,
@@ -194,7 +291,7 @@
         scratch_shapes=[pltpu.VMEM((65536, 128), F32), pltpu.VMEM((256, 128), F32)],
         compiler_params=pltpu.CompilerParams(vmem_limit_bytes=VMEM_LIMIT),
         name="y_pick",
-    )(data.reshape(256, 32, 128), rows, jnp.asarray(hi), jnp.asarray(lo))
+    )(data.reshape(8192, 128), rows, jnp.asarray(hi), jnp.asarray(lo))
 
 
 def turn_kernel(weights, out):
@@ -266,10 +363,7 @@
 def local(coil_images, send_lists, seg_slots, weights, counts):
     rows = table_rows(send_lists, seg_slots)
     turned = turn_weights(weights)
-    spectrum = z_transform(coil_images).reshape(8, 1024, 128)
-    spectrum = lax.all_to_all(spectrum, "gx", 0, 0, tiled=True)
-    spectrum = x_transform(spectrum)
-    spectrum = lax.all_to_all(spectrum, "gy", 0, 0, tiled=True)
+    spectrum = grid_values(coil_images)
     sent = y_pick(spectrum, rows)
     got = lax.all_to_all(sent, ("gx", "gy"), 0, 0, tiled=True)
     sums = interpolate(got.reshape(8, 2, 8, 2, 2, 8, 128), turned)

time: 257 us -> 218 us (0.85)
  Pallas kernels: 93.5 us -> 155 us
  blocking collectives: 57.1 us -> 0 us
  waiting for transfers between devices: 61 us -> 22.6 us
  starting transfers between devices: 32.3 us -> 26.8 us
    pallas_call x2 -> x1, Pallas kernels: 19.1 us -> 81 us  [grid_values(): pl.pallas_call(grid_kernel, out_shape=jax.ShapeDtypeStruct((4, 16, 16, 8,...]
    all_to_all x1 -> x0, blocking collectives: 57.1 us -> none  [local(): spectrum = lax.all_to_all(spectrum, 'gy', 0, 0, tiled=True)]
    all_to_all x1 -> x0, waiting for transfers between devices: 47.2 us -> none  [local(): spectrum = lax.all_to_all(spectrum, 'gx', 0, 0, tiled=True)]
    all_to_all x1, waiting for transfers between devices: 0.01 us -> 8.78 us  [table_rows(): lax.all_to_all(send_lists[0], both, 0, 0, tiled=True).reshape(1, 512)]
    all_to_all x1 -> x0, starting transfers between devices: 5.63 us -> none  [local(): spectrum = lax.all_to_all(spectrum, 'gx', 0, 0, tiled=True)]
    all_to_all x1, starting transfers between devices: 7.46 us -> 10.8 us  [local(): got = lax.all_to_all(sent, ('gx', 'gy'), 0, 0, tiled=True)]
    all_to_all x1, starting transfers between devices: 7.72 us -> 4.5 us  [table_rows(): return lax.all_to_all(sent, both, 0, 0, tiled=True).reshape(-1)]
    unnamed x21 -> x17, local copies, waits for them, and re-layouts: 8.23 us -> 7.85 us
  transfers between devices with their start and end apart: 4 -> 3, of which waited for: 2 -> 2; matrix products, arithmetic and copies ran while one was open for 1% -> 0% of each run, Pallas kernels for 14% -> 44%
where the time goes in v3:
time: 218 us; the launch traced here: 217 us
  Pallas kernels  155 us (71%)
  starting transfers between devices  26.8 us (12%)
  waiting for transfers between devices  22.6 us (10%)
  local copies, waits for them, and re-layouts  10.8 us (5%)
    pallas_call x1, Pallas kernels, grid_values(): pl.pallas_call(grid_kernel, out_shape=jax.ShapeDtypeStruct((4, 16, 16, 8,...  81 us
    pallas_call x1, Pallas kernels, y_pick(): pl.pallas_call(pick_kernel, out_shape=jax.ShapeDtypeStruct((128, 2, 16, 1...  51.7 us
    pallas_call x1, Pallas kernels, turn_weights(): pl.pallas_call(turn_kernel, out_shape=jax.ShapeDtypeStruct((2, 16, 512, 1...  15.6 us
    all_to_all x1, waiting for transfers between devices, local(): got = lax.all_to_all(sent, ('gx', 'gy'), 0, 0, tiled=True)  13.8 us
    all_to_all x1, starting transfers between devices, table_rows(): lax.all_to_all(send_lists[0], both, 0, 0, tiled=True).reshape(1, 512)  11.5 us
    all_to_all x1, starting transfers between devices, local(): got = lax.all_to_all(sent, ('gx', 'gy'), 0, 0, tiled=True)  10.8 us
    all_to_all x1, waiting for transfers between devices, table_rows(): lax.all_to_all(send_lists[0], both, 0, 0, tiled=True).reshape(1, 512)  8.78 us
    unnamed x17, local copies, waits for them, and re-layouts  7.85 us
  transfers between devices with their start and end apart: 3, of which 2 were waited for; matrix products, arithmetic and copies ran while one was open for 0% of the time, Pallas kernels for 44%

profile of v3, /device:TPU:1, one launch (start us, length us, event | category | flops | bytes accessed | tf_op | source)
XLA Modules:
  0.0 217.0 jit_solution(13027006207595549322)
XLA Ops:
  0.0 1.4 copy.17
  1.4 11.5 %all-to-all-start = ((s32[128,1,4]{2,1,0:T(1,128)}), s32[128,1,4]{2,1,0:T(1,128)S(1)}, u32[]{:S(2)}, u32[]{:S(2)}) async-start(s32[128,1,4]{2,1,0:T(1,128)} %bitcast.2), calls=%async_computation | async-start | bytes 131072 | tf_op jit(solution)/shard_map/all_to_all | solution.py:355
  12.9 0.8 eq.15
  13.7 8.8 %all-to-all-done = s32[128,1,4]{2,1,0:T(1,128)S(1)} async-done(((s32[128,1,4]{2,1,0:T(1,128)}), s32[128,1,4]{2,1,0:T(1,128)S(1)}, u32[]{:S(2)}, u32[]{:S(2)}) %all-to-all-start) | async-done | bytes 2080 | tf_op jit(solution)/shard_map/all_to_all | solution.py:355
  22.5 0.5 broadcast.49
  23.0 0.8 reduce.3
  23.8 0.1 broadcast_in_dim.36
  23.9 0.2 select_reduce_fusion
  24.1 0.7 broadcast_in_dim.39
  24.8 4.5 %all-to-all-start.1 = ((s32[128,1,256]{2,1,0:T(1,128)}), s32[128,1,256]{2,1,0:T(1,128)S(1)}, u32[]{:S(2)}, u32[]{:S(2)}) async-start(s32[128,1,256]{2,1,0:T(1,128)} %broadcast_in_dim.39), calls=%async_computation.1 | async-start | bytes 262144 | tf_op jit(solution)/shard_map/all_to_all | solution.py:360
  29.3 1.6 copy-done.1
  30.9 1.6 copy-done.2
  32.5 0.9 copy-done.5
  33.5 0.9 copy-done.6
  34.4 81.0 %grid_values.1 = f32[4,16,16,8,128]{4,3,2,1,0:T(8,128)} custom-call(f32[2,2,1024,256]{3,2,1,0:T(8,128)} %bitcast.15, bf16[256,512]{1,0:T(8,128)(2,1)S(1)} %copy-done.5, bf16[256,512]{1,0:T(8,128)(2,1)S(1)} %copy-done.6, bf16[1024,1024]{1,0:T(8,128)(2,1)S(1)} %copy-done.1, bf16[1024,1024]{1,0:T(8,128)(2,1)S(1)} %copy-done.2), custom_call_target="tpu_custom_call" | custom-call | tf_op jit(solution)/shard_map/grid_values/pallas_call | solution.py:198
  115.4 51.7 %y_pick.1 = f32[128,2,16,128]{3,2,1,0:T(8,128)S(1)} custom-call(f32[8192,128]{1,0:T(8,128)} %bitcast.13, s32[32768]{0:T(1024)S(1)} %bitcast.12, bf16[512,512]{1,0:T(8,128)(2,1)S(1)} %copy-done.3, bf16[512,512]{1,0:T(8,128)(2,1)S(1)} %copy-done.4), custom_call_target="tpu_custom_call" | custom-call | tf_op jit(solution)/shard_map/y_pick/pallas_call | solution.py:280
  167.2 1.4 copy-done
  168.5 10.8 %all-to-all-start.2 = ((f32[128,2,16,128]{3,2,1,0:T(8,128)}), f32[128,2,16,128]{3,2,1,0:T(8,128)S(1)}, u32[]{:S(2)}, u32[]{:S(2)}) async-start(f32[128,2,16,128]{3,2,1,0:T(8,128)} %copy-done), calls=%async_computation.2 | async-start | bytes 4194304 | tf_op jit(solution)/shard_map/all_to_all | solution.py:368
  179.4 15.6 %turn_weights.1.weights = f32[2,16,512,128]{3,2,1,0:T(8,128)} custom-call(f32[2,2048,512]{2,1,0:T(8,128)} %bitcast.14), custom_call_target="tpu_custom_call" | custom-call | tf_op jit(solution)/shard_map/turn_weights/pallas_call | solution.py:310
  195.0 13.8 %all-to-all-done.2 = f32[128,2,16,128]{3,2,1,0:T(8,128)S(1)} async-done(((f32[128,2,16,128]{3,2,1,0:T(8,128)}), f32[128,2,16,128]{3,2,1,0:T(8,128)S(1)}, u32[]{:S(2)}, u32[]{:S(2)}) %all-to-all-start.2) | async-done | bytes 2097184 | tf_op jit(solution)/shard_map/all_to_all | solution.py:368
  208.8 7.0 %interpolate.1 = f32[2,4,16,128]{3,2,1,0:T(8,128)S(1)} custom-call(f32[8,2,8,2,2,8,128]{6,5,4,3,2,1,0:T(8,128)S(1)} %bitcast.11, f32[2,16,512,128]{3,2,1,0:T(8,128)} %turn_weights.1.weights), custom_call_target="tpu_custom_call" | custom-call | tf_op jit(solution)/shard_map/interpolate/pallas_call | solution.py:339
  215.8 0.2 reshape.72
  216.0 0.3 reduce_sum.19
  216.4 0.6 copy.19
  (16 shorter events, 0.2 us)
Async XLA Ops:
  1.4 21.1 %all-to-all-start = ((s32[128,1,4]{2,1,0:T(1,128)}), s32[128,1,4]{2,1,0:T(1,128)S(1)}, u32[]{:S(2)}, u32[]{:S(2)}) async-start(s32[128,1,4]{2,1,0:T(1,128)} %bitcast.2), calls=%async_computation | async-start | bytes 131072 | tf_op jit(solution)/shard_map/all_to_all | solution.py:355
  24.8 90.6 %all-to-all-start.1 = ((s32[128,1,256]{2,1,0:T(1,128)}), s32[128,1,256]{2,1,0:T(1,128)S(1)}, u32[]{:S(2)}, u32[]{:S(2)}) async-start(s32[128,1,256]{2,1,0:T(1,128)} %broadcast_in_dim.39), calls=%async_computation.1 | async-start | bytes 262144 | tf_op jit(solution)/shard_map/all_to_all | solution.py:360
  29.3 1.6 copy-start.1
  30.9 1.6 copy-start.2
  32.5 0.9 copy-start.5
  33.5 0.9 copy-start.6
  34.4 81.0 %copy-start.3 = (bf16[512,512]{1,0:T(8,128)(2,1)S(1)}, bf16[512,512]{1,0:T(8,128)(2,1)}, u32[]{:S(2)}) copy-start(bf16[512,512]{1,0:T(8,128)(2,1)} %constant.30.clone.hi) | copy-start | bytes 1572868
  34.4 81.0 %copy-start.4 = (bf16[512,512]{1,0:T(8,128)(2,1)S(1)}, bf16[512,512]{1,0:T(8,128)(2,1)}, u32[]{:S(2)}) copy-start(bf16[512,512]{1,0:T(8,128)(2,1)} %constant.31.clone.lo) | copy-start | bytes 1572868
  167.2 1.4 copy-start
  168.5 40.3 %all-to-all-start.2 = ((f32[128,2,16,128]{3,2,1,0:T(8,128)}), f32[128,2,16,128]{3,2,1,0:T(8,128)S(1)}, u32[]{:S(2)}, u32[]{:S(2)}) async-start(f32[128,2,16,128]{3,2,1,0:T(8,128)} %copy-done), calls=%async_computation.2 | async-start | bytes 4194304 | tf_op jit(solution)/shard_map/all_to_all | solution.py:368
  179.4 15.6 %copy-start.7 = (s32[16]{0:T(128)S(1)}, s32[16]{0:T(128)}, u32[]{:S(2)}) copy-start(s32[16]{0:T(128)} %param.15) | copy-start | bytes 196

commit v4 on v3

--- a/solution.py
+++ b/solution.py
@@ -83,10 +83,61 @@
         sent[:, :, c, 2 * yp + k] = part
 
 
+def hops(pairs, axis, size, sems):
+    me = lax.axis_index(axis)
+    src, dst = pairs
+    made = []
+    for r in range(1, size):
+        to = (me + r) % size
+        made.append(
+            pltpu.make_async_remote_copy(
+                src_ref=src(to),
+                dst_ref=dst,
+                send_sem=sems.at[0, r],
+                recv_sem=sems.at[1, r],
+                device_id={axis: to},
+            )
+        )
+    return made
+
+
+def own_rows(listed, slots, mine, gy):
+    lists = listed[...].reshape(128, 128).astype(F32)
+    lists = pltpu.roll(lists, 64 - 4 * gy, 1)
+    row = lax.broadcasted_iota(jnp.int32, (128, 128), 0)
+    first = row % 8 * 64 + row // 8 * 4
+    for h in range(2):
+        wanted = slots[h : h + 1, :]
+        total = jnp.zeros((1, 128), F32)
+        for k in range(4):
+            column = jnp.broadcast_to(lists[:, 64 + k : 65 + k], (128, 128))
+            hit = first + k == wanted
+            total += jnp.sum(jnp.where(hit, column, 0.0), 0, keepdims=True)
+        ids = total.astype(jnp.int32)
+        low, high = jnp.bitwise_and(ids, 31), jnp.right_shift(ids, 5)
+        rows = low * 2048 + jnp.bitwise_and(high, 31) * 64 + jnp.right_shift(high, 5)
+        mine[h : h + 1, :] = rows
+
+
+def turn_unit(block, turned):
+    def one(n, carry):
+        part = block[pl.ds(n, 128, stride=16), :].T
+        for u in range(2):
+            for v in range(8):
+                at = (u * 8 + v) * 8
+                turned[n, pl.ds(u * 64 + v, 8, stride=8), :] = part[at : at + 8]
+        return carry
+
+    lax.fori_loop(0, 16, one, 0)
+
+
 def grid_kernel(
-    images, z_hi_in, z_lo_in, x_hi_in, x_lo_in, out,
+    images, z_hi_in, z_lo_in, x_hi_in, x_lo_in, lists, slots, weights,
+    out, rows_out, turned_out,
     image, z_hi, z_lo, x_hi, x_lo, z_out, x_in, x_out,
+    near, near8, listed, mine, mine8, block, turned,
     load_sem, self_sem, send1, recv1, send2, recv2,
+    small1, small2, small3, small4, block_sem, turned_sem,
 ):
     gx, gy = lax.axis_index("gx"), lax.axis_index("gy")
     loads = [
@@ -138,6 +189,25 @@
     def own_y(k):
         return pltpu.make_async_copy(x_out.at[k, gy], out.at[k, gy], self_sem.at[1, k])
 
+    hop1 = hops((lambda to: lists.at[to], near.at[gx]), "gx", GX, small1)
+    hop2 = hops((lambda to: near8, listed.at[gy]), "gy", GY, small2)
+    hop3 = hops((lambda to: mine, mine8.at[gx]), "gx", GX, small3)
+    hop4 = hops((lambda to: mine8, rows_out.at[gy]), "gy", GY, small4)
+    own4 = pltpu.make_async_copy(mine8, rows_out.at[gy], self_sem.at[2, 0])
+
+    def fetch(j, slot):
+        src = weights.at[j // 4, :, pl.ds(j % 4 * 128, 128)]
+        return pltpu.make_async_copy(src, block.at[slot], block_sem.at[slot])
+
+    def put(j, slot):
+        dst = turned_out.at[j // 4, :, pl.ds(j % 4 * 128, 128), :]
+        return pltpu.make_async_copy(turned.at[slot], dst, turned_sem.at[slot])
+
+    for hop in hop1:
+        hop.start()
+    for slot in range(2):
+        fetch(slot, slot).start()
+
     for load in loads[:2]:
         load.wait()
     for c in range(2):
@@ -160,7 +230,30 @@
 
     lax.fori_loop(0, 4, send_x, 0)
 
+    near[gx] = lists[gx]
+    for hop in hop1:
+        hop.wait()
+    for a in range(GX):
+        near8[a : a + 1, :] = near[a]
+    for hop in hop2:
+        hop.start()
+    listed[gy] = near8[...]
+
     def chunk(k, carry):
+        for slot in range(2):
+            fetch(2 * k + slot, slot).wait()
+
+            @pl.when(k > 0)
+            def _():
+                put(2 * k + slot - 2, slot).wait()
+
+            turn_unit(block.at[slot], turned.at[slot])
+            put(2 * k + slot, slot).start()
+
+            @pl.when(k < 3)
+            def _():
+                fetch(2 * k + slot + 2, slot).start()
+
         own_x(k).wait()
         for r in range(1, GX):
             over_x(k, r).wait_recv()
@@ -176,9 +269,32 @@
         for r in range(1, GY):
             over_y(k, r).start()
         own_y(k).start()
+
+        @pl.when(k == 0)
+        def _():
+            for hop in hop2:
+                hop.wait()
+            own_rows(listed, slots, mine, gy)
+            for hop in hop3:
+                hop.start()
+            mine8[gx] = mine[...]
+
+        @pl.when(k == 1)
+        def _():
+            for hop in hop3:
+                hop.wait()
+            for hop in hop4:
+                hop.start()
+            own4.start()
+
         return carry
 
     lax.fori_loop(0, 4, chunk, 0)
+    for hop in hop4:
+        hop.wait()
+    own4.wait()
+    for slot in range(2):
+        put(6 + slot, slot).wait()
 
     def finish(k, carry):
         own_y(k).wait()
@@ -191,15 +307,21 @@
     lax.fori_loop(0, 4, finish, 0)
 
 
-def grid_values(images):
+def grid_values(images, lists, slots, weights):
     tables = [jnp.asarray(t) for t in z_table() + x_table()]
     anywhere = pl.BlockSpec(memory_space=pl.ANY)
-    sems = pltpu.SemaphoreType.DMA
+    inside = pl.BlockSpec(memory_space=pltpu.VMEM)
+    dma = pltpu.SemaphoreType.DMA
+    i32 = jnp.int32
     return pl.pallas_call(
         grid_kernel,
-        out_shape=jax.ShapeDtypeStruct((4, 16, 16, 8, 128), F32),
-        in_specs=[anywhere] * 5,
-        out_specs=anywhere,
+        out_shape=(
+            jax.ShapeDtypeStruct((4, 16, 16, 8, 128), F32),
+            jax.ShapeDtypeStruct((GY, GX, 2, 128), i32),
+            jax.ShapeDtypeStruct((2, 16, 512, 128), F32),
+        ),
+        in_specs=[anywhere] * 5 + [inside] * 2 + [anywhere],
+        out_specs=(anywhere,) * 3,
         scratch_shapes=[
             pltpu.VMEM((2, 2, 2, 1024, 128), F32),
             pltpu.VMEM((256, 512), BF16),
@@ -209,18 +331,31 @@
             pltpu.VMEM((4, 8, 2, 16, 8, 128), F32),
             pltpu.VMEM((4, 8, 2, 16, 8, 128), F32),
             pltpu.VMEM((4, 16, 16, 8, 128), F32),
-            sems((12,)),
-            sems((2, 4)),
-            sems((4, GX)),
-            sems((4, GX)),
-            sems((4, GY)),
-            sems((4, GY)),
+            pltpu.VMEM((GX, 1, 128), i32),
+            pltpu.VMEM((GX, 128), i32),
+            pltpu.VMEM((GY, GX, 128), i32),
+            pltpu.VMEM((2, 128), i32),
+            pltpu.VMEM((GX, 2, 128), i32),
+            pltpu.VMEM((2, 2048, 128), F32),
+            pltpu.VMEM((2, 16, 128, 128), F32),
+            dma((12,)),
+            dma((3, 4)),
+            dma((4, GX)),
+            dma((4, GX)),
+            dma((4, GY)),
+            dma((4, GY)),
+            dma((2, GX)),
+            dma((2, GY)),
+            dma((2, GX)),
+            dma((2, GY)),
+            dma((2,)),
+            dma((2,)),
         ],
         compiler_params=pltpu.CompilerParams(
             vmem_limit_bytes=VMEM_LIMIT, collective_id=0, has_side_effects=True
         ),
         name="grid_values",
-    )(images.reshape(2, 2, 1024, 256), *tables)
+    )(images, *tables, lists, slots, weights)
 
 
 def y_group(g, data, hi, lo, table):
@@ -245,12 +380,12 @@
     lax.fori_loop(0, 2, four, 0)
 
 
-def pick_group(rows, table, raw, out):
+def pick_group(bases, rows, table, raw, out):
     def eight(t, carry):
         for s in range(8):
             for g in range(8):
                 lanes = slice(g * 16, g * 16 + 16)
-                row = rows[g * 256 + t * 8 + s]
+                row = rows[bases[g] + t * 8 + s]
                 raw[pl.ds(t * 8 + s, 1), lanes] = table[pl.ds(row, 1), lanes]
         return carry
 
@@ -261,61 +396,97 @@
             out[g, h] = turned[g * 16 : (g + 1) * 16]
 
 
-def pick_kernel(data, rows, hi, lo, out, table, raw):
-    g = pl.program_id(0)
-
-    @pl.when(g < 4)
-    def _():
-        y_group(g, data, hi, lo, table)
-
-    @pl.when(g >= 4)
-    def _():
-        pick_group(rows, table, raw, out)
+def pick_kernel(data_in, rows, hi, lo, out, data, table, raw, sent, load_sem, self_sem, send, recv):
+    gx, gy = lax.axis_index("gx"), lax.axis_index("gy")
+    me = gx * GY + gy
+    loads = [
+        pltpu.make_async_copy(data_in.at[k], data.at[k], load_sem.at[k]) for k in range(4)
+    ]
+    for load in loads:
+        load.start()
+    barrier = pltpu.get_barrier_semaphore()
+
+    def greet(o, carry):
+        to = (me + o) % DEVS
+        pl.semaphore_signal(barrier, inc=1, device_id={"gx": to // GY, "gy": to % GY})
+        return carry
+
+    lax.fori_loop(1, DEVS, greet, 0)
+
+    for k in range(4):
+        loads[k].wait()
+        y_group(k, data.at[k], hi, lo, table)
+
+    pl.semaphore_wait(barrier, DEVS - 1)
+
+    def copy(i, g):
+        return pltpu.make_async_remote_copy(
+            src_ref=sent.at[i, g],
+            dst_ref=out.at[me],
+            send_sem=send.at[i, g],
+            recv_sem=recv.at[i, g],
+            device_id={"gx": (gx + g) % GX, "gy": (gy + i) % GY},
+        )
+
+    own = pltpu.make_async_copy(sent.at[0, 0], out.at[me], self_sem)
+
+    def group(i, carry):
+        to = (gy + i) % GY
+        bases = [to * 2048 + (gx + g) % GX * 256 for g in range(8)]
+        pick_group(bases, rows, table, raw, sent.at[i])
+
+        @pl.when(i == 0)
+        def _():
+            own.start()
+
+        @pl.when(i > 0)
+        def _():
+            copy(i, 0).start()
+
+        for g in range(1, 8):
+            copy(i, g).start()
+        return carry
+
+    lax.fori_loop(0, 16, group, 0)
+    own.wait()
+
+    def finish(i, carry):
+        @pl.when(i > 0)
+        def _():
+            copy(i, 0).wait()
+
+        for g in range(1, 8):
+            copy(i, g).wait()
+        return carry
+
+    lax.fori_loop(0, 16, finish, 0)
 
 
 def y_pick(data, rows):
     hi, lo = y_table()
-    whole = pl.BlockSpec((512, 512), lambda g: (0, 0))
-    late = lambda g: jnp.maximum(g - 4, 0)
+    anywhere = pl.BlockSpec(memory_space=pl.ANY)
+    inside = pl.BlockSpec(memory_space=pltpu.VMEM)
+    dma = pltpu.SemaphoreType.DMA
     return pl.pallas_call(
         pick_kernel,
         out_shape=jax.ShapeDtypeStruct((128, 2, 16, 128), F32),
-        grid=(20,),
-        in_specs=[
-            pl.BlockSpec((2048, 128), lambda g: (jnp.minimum(g, 3), 0)),
-            pl.BlockSpec((2048,), lambda g: (late(g),), memory_space=pltpu.SMEM),
-            whole,
-            whole,
+        in_specs=[anywhere, pl.BlockSpec(memory_space=pltpu.SMEM), inside, inside],
+        out_specs=anywhere,
+        scratch_shapes=[
+            pltpu.VMEM((4, 2048, 128), F32),
+            pltpu.VMEM((65536, 128), F32),
+            pltpu.VMEM((256, 128), F32),
+            pltpu.VMEM((16, 8, 2, 16, 128), F32),
+            dma((4,)),
+            dma,
+            dma((16, 8)),
+            dma((16, 8)),
         ],
-        out_specs=pl.BlockSpec((8, 2, 16, 128), lambda g: (late(g), 0, 0, 0)),
-        scratch_shapes=[pltpu.VMEM((65536, 128), F32), pltpu.VMEM((256, 128), F32)],
-        compiler_params=pltpu.CompilerParams(vmem_limit_bytes=VMEM_LIMIT),
+        compiler_params=pltpu.CompilerParams(
+            vmem_limit_bytes=VMEM_LIMIT, collective_id=1, has_side_effects=True
+        ),
         name="y_pick",
-    )(data.reshape(8192, 128), rows, jnp.asarray(hi), jnp.asarray(lo))
-
-
-def turn_kernel(weights, out):
-    def one(n, carry):
-        turned = weights[0, pl.ds(n, 128, stride=16), :].T
-        for u in range(2):
-            for v in range(8):
-                at = (u * 8 + v) * 8
-                out[0, n, pl.ds(u * 64 + v, 8, stride=8), :] = turned[at : at + 8]
-        return carry
-
-    lax.fori_loop(0, 16, one, 0)
-
-
-def turn_weights(weights):
-    return pl.pallas_call(
-        turn_kernel,
-        out_shape=jax.ShapeDtypeStruct((2, 16, 512, 128), F32),
-        grid=(2, 4),
-        in_specs=[pl.BlockSpec((1, 2048, 128), lambda h, e: (h, 0, e))],
-        out_specs=pl.BlockSpec((1, 16, 128, 128), lambda h, e: (h, 0, e, 0)),
-        compiler_params=pltpu.CompilerParams(vmem_limit_bytes=VMEM_LIMIT),
-        name="turn_weights",
-    )(weights.reshape(2, 2048, 512))
+    )(data, rows, jnp.asarray(hi), jnp.asarray(lo))
 
 
 def sum_kernel(got, weights, out):
@@ -350,22 +521,15 @@
     )(got, weights)
 
 
-def table_rows(send_lists, seg_slots):
-    both = ("gx", "gy")
-    lists = lax.all_to_all(send_lists[0], both, 0, 0, tiled=True).reshape(1, 512)
-    hit = seg_slots.reshape(256, 1) == jnp.arange(512, dtype=jnp.int32)[None, :]
-    ids = jnp.sum(jnp.where(hit, lists, 0), 1)
-    rows = (ids & 31) * 2048 + ((ids >> 5) & 31) * 64 + (ids >> 10)
-    sent = jnp.broadcast_to(rows[None, :], (DEVS, 256))
-    return lax.all_to_all(sent, both, 0, 0, tiled=True).reshape(-1)
-
-
 def local(coil_images, send_lists, seg_slots, weights, counts):
-    rows = table_rows(send_lists, seg_slots)
-    turned = turn_weights(weights)
-    spectrum = grid_values(coil_images)
-    sent = y_pick(spectrum, rows)
-    got = lax.all_to_all(sent, ("gx", "gy"), 0, 0, tiled=True)
+    lists = jnp.pad(send_lists.reshape(GX, 1, 64), ((0, 0), (0, 0), (0, 64)))
+    values, rows, turned = grid_values(
+        coil_images.reshape(2, 2, 1024, 256),
+        lists,
+        seg_slots.reshape(2, 128),
+        weights.reshape(2, 2048, 512),
+    )
+    got = y_pick(values.reshape(4, 2048, 128), rows.reshape(-1))
     sums = interpolate(got.reshape(8, 2, 8, 2, 2, 8, 128), turned)
     sums = sums.reshape(2, 16, 2, 2, 8, 16).sum(-1)
     samples = sums.transpose(0, 4, 2, 3, 1).reshape(16, 2, 2, 16)

time: 218 us -> 187 us (0.86)
  starting transfers between devices: 26.8 us -> 0 us
  Pallas kernels: 155 us -> 179 us
  waiting for transfers between devices: 22.6 us -> 0 us
  local copies, waits for them, and re-layouts: 10.8 us -> 7.66 us
    all_to_all x3 -> x0, starting transfers between devices: 26.8 us -> none  [the longest x1 11.5 us: table_rows(): lax.all_to_all(send_lists[0], both, 0, 0, tiled=True).reshape(1, 512)]
    all_to_all x3 -> x0, waiting for transfers between devices: 22.6 us -> none  [the longest x1 13.8 us: local(): got = lax.all_to_all(sent, ('gx', 'gy'), 0, 0, tiled=True)]
    pallas_call x1, Pallas kernels: 51.7 us -> 72.2 us  [y_pick(): pl.pallas_call(pick_kernel, out_shape=jax.ShapeDtypeStruct((128, 2, 16, 1...]
    pallas_call x2 -> x1, Pallas kernels: 96.6 us -> 99.5 us  [grid_values(): pl.pallas_call(grid_kernel, out_shape=(jax.ShapeDtypeStruct((4, 16, 16, 8...]
    unnamed x17 -> x15, local copies, waits for them, and re-layouts: 7.85 us -> 5.88 us
  transfers between devices with their start and end apart: 3 -> 0, of which waited for: 2 -> 0; matrix products, arithmetic and copies ran while one was open for 0% -> 0% of each run, Pallas kernels for 44% -> 0%
where the time goes in v4:
time: 187 us
  Pallas kernels  179 us (96%)
  local copies, waits for them, and re-layouts  7.66 us (4%)
    pallas_call x1, Pallas kernels, grid_values(): pl.pallas_call(grid_kernel, out_shape=(jax.ShapeDtypeStruct((4, 16, 16, 8...  99.5 us
    pallas_call x1, Pallas kernels, y_pick(): pl.pallas_call(pick_kernel, out_shape=jax.ShapeDtypeStruct((128, 2, 16, 1...  72.2 us
    pallas_call x1, Pallas kernels, interpolate(): pl.pallas_call(sum_kernel, out_shape=jax.ShapeDtypeStruct((2, 4, 16, 128)...  7.01 us
    unnamed x15, local copies, waits for them, and re-layouts  5.88 us

profile of v4, /device:TPU:1, one launch (start us, length us, event | category | flops | bytes accessed | tf_op | source)
XLA Modules:
  0.0 186.8 jit_solution(13543561218440311436)
XLA Ops:
  0.0 0.8 copy.17
  0.8 0.1 reshape.49
  0.9 0.8 reshape.50.slots
  1.7 0.0 copy-start
  1.7 1.6 copy-done
  3.3 0.0 copy-start.1
  3.3 1.6 copy-done.1
  4.9 0.0 copy-start.4
  4.9 0.9 copy-done.4
  5.8 0.0 copy-start.5
  5.8 0.9 copy-done.5
  6.8 0.0 copy-start.2
  6.8 99.5 %grid_values.1 = (f32[4,16,16,8,128]{4,3,2,1,0:T(8,128)}, s32[16,8,2,128]{3,2,1,0:T(2,128)S(1)}, f32[2,16,512,128]{3,2,1,0:T(8,128)}) custom-call(f32[2,2,1024,256]{3,2,1,0:T(8,128)} %bitcast.14, bf16[256,512]{1,0:T(8,128)(2,1)S(1)} %copy-done.4, bf16[256,512]{1,0:T(8,128)(2,1)S(1)} %copy-done.5, bf16[1024,1024]{1,0:T(8,128)(2,1)S(1)} %copy-done, ...), custom_call_target="tpu_custom_call" | custom-call | tf_op jit(solution)/shard_map/grid_values/pallas_call | solution.py:316
  106.2 0.0 copy-done.2
  106.2 0.0 copy-done.3
  106.2 72.2 %y_pick.1 = f32[128,2,16,128]{3,2,1,0:T(8,128)S(1)} custom-call(f32[4,2048,128]{2,1,0:T(8,128)} %bitcast.15, s32[32768]{0:T(1024)S(1)} %bitcast.12, bf16[512,512]{1,0:T(8,128)(2,1)S(1)} %copy-done.2, bf16[512,512]{1,0:T(8,128)(2,1)S(1)} %copy-done.3), custom_call_target="tpu_custom_call" | custom-call | tf_op jit(solution)/shard_map/y_pick/pallas_call | solution.py:470
  178.5 0.0 copy-start.6
  178.5 7.0 %interpolate.1 = f32[2,4,16,128]{3,2,1,0:T(8,128)S(1)} custom-call(f32[8,2,8,2,2,8,128]{6,5,4,3,2,1,0:T(8,128)S(1)} %bitcast.11, f32[2,16,512,128]{3,2,1,0:T(8,128)} %get-tuple-element.10.weights), custom_call_target="tpu_custom_call" | custom-call | tf_op jit(solution)/shard_map/interpolate/pallas_call | solution.py:510
  185.5 0.2 reshape.55
  185.7 0.3 reduce_sum.9
  186.0 0.1 copy.19
  186.1 0.0 copy-done.6
  186.1 0.1 iota_compare_fusion
  186.2 0.6 copy.20
  (3 shorter events, 0.0 us)
Async XLA Ops:
  1.7 1.6 copy-start
  3.3 1.6 copy-start.1
  4.9 0.9 copy-start.4
  5.8 0.9 copy-start.5
  6.8 99.5 %copy-start.2 = (bf16[512,512]{1,0:T(8,128)(2,1)S(1)}, bf16[512,512]{1,0:T(8,128)(2,1)}, u32[]{:S(2)}) copy-start(bf16[512,512]{1,0:T(8,128)(2,1)} %constant.20.clone.hi) | copy-start | bytes 1572868
  6.8 99.5 %copy-start.3 = (bf16[512,512]{1,0:T(8,128)(2,1)S(1)}, bf16[512,512]{1,0:T(8,128)(2,1)}, u32[]{:S(2)}) copy-start(bf16[512,512]{1,0:T(8,128)(2,1)} %constant.21.clone.lo) | copy-start | bytes 1572868
  178.5 7.6 %copy-start.6 = (s32[16]{0:T(128)S(1)}, s32[16]{0:T(128)}, u32[]{:S(2)}) copy-start(s32[16]{0:T(128)} %param.15) | copy-start | bytes 196

commit v5 on v4

--- a/solution.py
+++ b/solution.py
@@ -13,7 +13,7 @@
 GX, GY = 8, 16
 DEVS = GX * GY
 F32, BF16 = jnp.float32, jnp.bfloat16
-VMEM_LIMIT = 48 * 2**20
+WIDE_VMEM = 62 * 2**20
 
 
 def split_table(table):
@@ -80,7 +80,9 @@
     res = dot3((hi[...], lo[...]), halves(data), ((1,), (1,)))
     for k in range(2):
         part = res[:, k * 128 : (k + 1) * 128].reshape(4, 8, 8, 128)
-        sent[:, :, c, 2 * yp + k] = part
+        y = 2 * yp + k
+        for b in range(4):
+            sent[y // 8 * 4 + b, :, c, y % 8] = part[b]
 
 
 def hops(pairs, axis, size, sems):
@@ -103,14 +105,14 @@
 
 def own_rows(listed, slots, mine, gy):
     lists = listed[...].reshape(128, 128).astype(F32)
-    lists = pltpu.roll(lists, 64 - 4 * gy, 1)
+    lists = pltpu.roll(lists, (128 - gy) % 128, 1)
     row = lax.broadcasted_iota(jnp.int32, (128, 128), 0)
     first = row % 8 * 64 + row // 8 * 4
     for h in range(2):
         wanted = slots[h : h + 1, :]
         total = jnp.zeros((1, 128), F32)
         for k in range(4):
-            column = jnp.broadcast_to(lists[:, 64 + k : 65 + k], (128, 128))
+            column = jnp.broadcast_to(lists[:, 16 * k : 16 * k + 1], (128, 128))
             hit = first + k == wanted
             total += jnp.sum(jnp.where(hit, column, 0.0), 0, keepdims=True)
         ids = total.astype(jnp.int32)
@@ -163,37 +165,35 @@
         pl.semaphore_signal(barrier, inc=1, device_id={"gy": (gy + r) % GY})
     pl.semaphore_wait(barrier, GX + GY - 2)
 
-    def over_x(k, r):
+    def over_x(m, r):
         to = (gx + r) % GX
         return pltpu.make_async_remote_copy(
-            src_ref=z_out.at[k, to],
-            dst_ref=x_in.at[k, gx],
-            send_sem=send1.at[k, r],
-            recv_sem=recv1.at[k, r],
+            src_ref=z_out.at[m, to],
+            dst_ref=x_in.at[m, gx],
+            send_sem=send1.at[m, r],
+            recv_sem=recv1.at[m, r],
             device_id={"gx": to},
         )
 
-    def over_y(k, r):
+    def over_y(m, r):
         to = (gy + r) % GY
         return pltpu.make_async_remote_copy(
-            src_ref=x_out.at[k, to],
-            dst_ref=out.at[k, gy],
-            send_sem=send2.at[k, r],
-            recv_sem=recv2.at[k, r],
+            src_ref=x_out.at[m, to],
+            dst_ref=out.at[m % 4, gy, pl.ds(m // 4 * 8, 8)],
+            send_sem=send2.at[m, r],
+            recv_sem=recv2.at[m, r],
             device_id={"gy": to},
         )
 
-    def own_x(k):
-        return pltpu.make_async_copy(z_out.at[k, gx], x_in.at[k, gx], self_sem.at[0, k])
-
-    def own_y(k):
-        return pltpu.make_async_copy(x_out.at[k, gy], out.at[k, gy], self_sem.at[1, k])
-
-    hop1 = hops((lambda to: lists.at[to], near.at[gx]), "gx", GX, small1)
+    def own_y(m):
+        dst = out.at[m % 4, gy, pl.ds(m // 4 * 8, 8)]
+        return pltpu.make_async_copy(x_out.at[m, gy], dst, self_sem.at[m])
+
+    hop1 = hops((lambda to: lists, near.at[gx]), "gx", GX, small1)
     hop2 = hops((lambda to: near8, listed.at[gy]), "gy", GY, small2)
     hop3 = hops((lambda to: mine, mine8.at[gx]), "gx", GX, small3)
     hop4 = hops((lambda to: mine8, rows_out.at[gy]), "gy", GY, small4)
-    own4 = pltpu.make_async_copy(mine8, rows_out.at[gy], self_sem.at[2, 0])
+    own4 = pltpu.make_async_copy(mine8, rows_out.at[gy], self_sem.at[8])
 
     def fetch(j, slot):
         src = weights.at[j // 4, :, pl.ds(j % 4 * 128, 128)]
@@ -203,113 +203,114 @@
         dst = turned_out.at[j // 4, :, pl.ds(j % 4 * 128, 128), :]
         return pltpu.make_async_copy(turned.at[slot], dst, turned_sem.at[slot])
 
+    def z_half(half):
+        for c in range(2):
+            if half == 0:
+                for load in loads[2 + 4 * c : 6 + 4 * c]:
+                    load.wait()
+
+            def pair(yp, carry):
+                z_pair(yp + 4 * half, c, image, z_hi, z_lo, z_out)
+                return carry
+
+            lax.fori_loop(0, 4, pair, 0)
+
+    def send_x(half):
+        def one(m, carry):
+            for r in range(1, GX):
+                over_x(m, r).start()
+            return carry
+
+        lax.fori_loop(4 * half, 4 * half + 4, one, 0)
+
     for hop in hop1:
         hop.start()
-    for slot in range(2):
-        fetch(slot, slot).start()
-
+    near[gx] = lists[...]
     for load in loads[:2]:
         load.wait()
-    for c in range(2):
-        for load in loads[2 + 4 * c : 6 + 4 * c]:
-            load.wait()
-
-        def pair(yp, carry):
-            z_pair(yp, c, image, z_hi, z_lo, z_out)
-            return carry
-
-        lax.fori_loop(0, 8, pair, 0)
-    for load in loads[10:]:
-        load.wait()
-
-    def send_x(k, carry):
-        for r in range(1, GX):
-            over_x(k, r).start()
-        own_x(k).start()
-        return carry
-
-    lax.fori_loop(0, 4, send_x, 0)
-
-    near[gx] = lists[gx]
+    z_half(0)
     for hop in hop1:
         hop.wait()
+    lane = lax.broadcasted_iota(jnp.int32, (1, 128), 1)
     for a in range(GX):
-        near8[a : a + 1, :] = near[a]
+        kept = jnp.zeros((1, 128), jnp.int32)
+        for k in range(4):
+            moved = pltpu.roll(near[a, k : k + 1, :], (128 + 16 * k - 16 * gx) % 128, 1)
+            kept = jnp.where(lane // 16 == k, moved, kept)
+        near8[a : a + 1, :] = kept
     for hop in hop2:
         hop.start()
     listed[gy] = near8[...]
-
-    def chunk(k, carry):
-        for slot in range(2):
-            fetch(2 * k + slot, slot).wait()
-
-            @pl.when(k > 0)
-            def _():
-                put(2 * k + slot - 2, slot).wait()
-
-            turn_unit(block.at[slot], turned.at[slot])
-            put(2 * k + slot, slot).start()
-
-            @pl.when(k < 3)
-            def _():
-                fetch(2 * k + slot + 2, slot).start()
-
-        own_x(k).wait()
+    send_x(0)
+    z_half(1)
+    for hop in hop2:
+        hop.wait()
+    own_rows(listed, slots, mine, gy)
+    for hop in hop3:
+        hop.start()
+    mine8[gx] = mine[...]
+    send_x(1)
+    for slot in range(2):
+        fetch(slot, slot).start()
+    for load in loads[10:]:
+        load.wait()
+    for hop in hop3:
+        hop.wait()
+    for hop in hop4:
+        hop.start()
+    own4.start()
+
+    def chunk(m, carry):
+        slot = m % 2
+        fetch(m, slot).wait()
+
+        @pl.when(m > 1)
+        def _():
+            put(m - 2, slot).wait()
+
+        turn_unit(block.at[slot], turned.at[slot])
+        put(m, slot).start()
+
+        @pl.when(m < 6)
+        def _():
+            fetch(m + 2, slot).start()
+
+        x_in[m, gx] = z_out[m, gx]
         for r in range(1, GX):
-            over_x(k, r).wait_recv()
-        rows = jnp.concatenate(
-            [x_in[k, a].reshape(256, 128) for a in range(8)], 1
-        )
+            over_x(m, r).wait_recv()
+        rows = jnp.concatenate([x_in[m, a].reshape(128, 128) for a in range(8)], 1)
         res = dot3(halves(rows), (x_hi[...], x_lo[...]), ((1,), (0,)))
         for c in range(2):
             for u in range(8):
-                x_out[k, c * 8 + u] = res[
-                    c * 128 : (c + 1) * 128, u * 128 : (u + 1) * 128
-                ].reshape(16, 8, 128)
+                x_out[m, c * 8 + u] = res[
+                    c * 64 : (c + 1) * 64, u * 128 : (u + 1) * 128
+                ].reshape(8, 8, 128)
         for r in range(1, GY):
-            over_y(k, r).start()
-        own_y(k).start()
-
-        @pl.when(k == 0)
-        def _():
-            for hop in hop2:
-                hop.wait()
-            own_rows(listed, slots, mine, gy)
-            for hop in hop3:
-                hop.start()
-            mine8[gx] = mine[...]
-
-        @pl.when(k == 1)
-        def _():
-            for hop in hop3:
-                hop.wait()
-            for hop in hop4:
-                hop.start()
-            own4.start()
-
-        return carry
-
-    lax.fori_loop(0, 4, chunk, 0)
+            over_y(m, r).start()
+        own_y(m).start()
+        return carry
+
+    lax.fori_loop(0, 8, chunk, 0)
     for hop in hop4:
         hop.wait()
     own4.wait()
     for slot in range(2):
         put(6 + slot, slot).wait()
 
-    def finish(k, carry):
-        own_y(k).wait()
+    def finish(m, carry):
+        own_y(m).wait()
         for r in range(1, GX):
-            over_x(k, r).wait_send()
+            over_x(m, r).wait_send()
         for r in range(1, GY):
-            over_y(k, r).wait()
-        return carry
-
-    lax.fori_loop(0, 4, finish, 0)
+            over_y(m, r).wait()
+        return carry
+
+    lax.fori_loop(0, 8, finish, 0)
 
 
 def grid_values(images, lists, slots, weights):
     tables = [jnp.asarray(t) for t in z_table() + x_table()]
-    anywhere = pl.BlockSpec(memory_space=pl.ANY)
+    hbm = pl.BlockSpec(memory_space=pltpu.HBM)
     inside = pl.BlockSpec(memory_space=pltpu.VMEM)
     dma = pltpu.SemaphoreType.DMA
     i32 = jnp.int32
@@ -320,18 +321,18 @@
             jax.ShapeDtypeStruct((GY, GX, 2, 128), i32),
             jax.ShapeDtypeStruct((2, 16, 512, 128), F32),
         ),
-        in_specs=[anywhere] * 5 + [inside] * 2 + [anywhere],
-        out_specs=(anywhere,) * 3,
+        in_specs=[hbm] * 5 + [inside] * 2 + [hbm],
+        out_specs=(hbm,) * 3,
         scratch_shapes=[
             pltpu.VMEM((2, 2, 2, 1024, 128), F32),
             pltpu.VMEM((256, 512), BF16),
             pltpu.VMEM((256, 512), BF16),
             pltpu.VMEM((1024, 1024), BF16),
             pltpu.VMEM((1024, 1024), BF16),
-            pltpu.VMEM((4, 8, 2, 16, 8, 128), F32),
-            pltpu.VMEM((4, 8, 2, 16, 8, 128), F32),
-            pltpu.VMEM((4, 16, 16, 8, 128), F32),
-            pltpu.VMEM((GX, 1, 128), i32),
+            pltpu.VMEM((8, 8, 2, 8, 8, 128), F32),
+            pltpu.VMEM((8, 8, 2, 8, 8, 128), F32),
+            pltpu.VMEM((8, 16, 8, 8, 128), F32),
+            pltpu.VMEM((GX, 4, 128), i32),
             pltpu.VMEM((GX, 128), i32),
             pltpu.VMEM((GY, GX, 128), i32),
             pltpu.VMEM((2, 128), i32),
@@ -339,11 +340,11 @@
             pltpu.VMEM((2, 2048, 128), F32),
             pltpu.VMEM((2, 16, 128, 128), F32),
             dma((12,)),
-            dma((3, 4)),
-            dma((4, GX)),
-            dma((4, GX)),
-            dma((4, GY)),
-            dma((4, GY)),
+            dma((9,)),
+            dma((8, GX)),
+            dma((8, GX)),
+            dma((8, GY)),
+            dma((8, GY)),
             dma((2, GX)),
             dma((2, GY)),
             dma((2, GX)),
@@ -352,7 +353,7 @@
             dma((2,)),
         ],
         compiler_params=pltpu.CompilerParams(
-            vmem_limit_bytes=VMEM_LIMIT, collective_id=0, has_side_effects=True
+            vmem_limit_bytes=WIDE_VMEM, collective_id=0, has_side_effects=True
         ),
         name="grid_values",
     )(images, *tables, lists, slots, weights)
@@ -483,7 +484,7 @@
             dma((16, 8)),
         ],
         compiler_params=pltpu.CompilerParams(
-            vmem_limit_bytes=VMEM_LIMIT, collective_id=1, has_side_effects=True
+            vmem_limit_bytes=WIDE_VMEM, collective_id=1, has_side_effects=True
         ),
         name="y_pick",
     )(data, rows, jnp.asarray(hi), jnp.asarray(lo))
@@ -516,13 +517,13 @@
             pl.BlockSpec((1, 4, 512, 128), lambda h, n: (h, n, 0, 0)),
         ],
         out_specs=pl.BlockSpec((1, 1, 16, 128), lambda h, n: (h, n, 0, 0)),
-        compiler_params=pltpu.CompilerParams(vmem_limit_bytes=VMEM_LIMIT),
+        compiler_params=pltpu.CompilerParams(vmem_limit_bytes=WIDE_VMEM),
         name="interpolate",
     )(got, weights)
 
 
 def local(coil_images, send_lists, seg_slots, weights, counts):
-    lists = jnp.pad(send_lists.reshape(GX, 1, 64), ((0, 0), (0, 0), (0, 64)))
+    lists = send_lists[0].T
     values, rows, turned = grid_values(
         coil_images.reshape(2, 2, 1024, 256),
         lists,

time: 187 us -> 181 us (0.968)
  local copies, waits for them, and re-layouts: 7.66 us -> 3.09 us
  Pallas kernels: 179 us -> 177 us
    unnamed x15 -> x2, local copies, waits for them, and re-layouts: 5.88 us -> 0.01 us
    pallas_call x1, Pallas kernels: 99.5 us -> 95.1 us  [grid_values(): pl.pallas_call(grid_kernel, out_shape=(jax.ShapeDtypeStruct((4, 16, 16, 8...]
where the time goes in v5:
time: 181 us; the launch traced here: 180 us
  Pallas kernels  177 us (98%)
  local copies, waits for them, and re-layouts  3.09 us (2%)
    pallas_call x1, Pallas kernels, grid_values(): pl.pallas_call(grid_kernel, out_shape=(jax.ShapeDtypeStruct((4, 16, 16, 8...  95.1 us
    pallas_call x1, Pallas kernels, y_pick(): pl.pallas_call(pick_kernel, out_shape=jax.ShapeDtypeStruct((128, 2, 16, 1...  73.5 us
    pallas_call x1, Pallas kernels, interpolate(): pl.pallas_call(sum_kernel, out_shape=jax.ShapeDtypeStruct((2, 4, 16, 128)...  8.32 us

profile of v5, /device:TPU:1, one launch (start us, length us, event | category | flops | bytes accessed | tf_op | source)
XLA Modules:
  0.0 180.4 jit_solution(12487529032982690368)
XLA Ops:
  0.0 1.3 reshape.46.slots
  1.3 95.1 %grid_values.1 = (f32[4,16,16,8,128]{4,3,2,1,0:T(8,128)}, s32[16,8,2,128]{3,2,1,0:T(2,128)}, f32[2,16,512,128]{3,2,1,0:T(8,128)}) custom-call(f32[2,2,1024,256]{3,2,1,0:T(8,128)} %bitcast.15, bf16[256,512]{1,0:T(8,128)(2,1)} %constant.14.clone.z_hi_in, bf16[256,512]{1,0:T(8,128)(2,1)} %constant.15.clone.z_lo_in, bf16[1024,1024]{1,0:T(8,128)(2,1)} %constant.16.clone.x_hi_in, ...), custom_call_target="tpu_custom_call" | custom-call | tf_op jit(solution)/shard_map/grid_values/pallas_call | solution.py:317
  96.5 73.5 %y_pick.1 = f32[128,2,16,128]{3,2,1,0:T(8,128)} custom-call(f32[4,2048,128]{2,1,0:T(8,128)} %bitcast.16, s32[32768]{0:T(1024)} %bitcast.18, bf16[512,512]{1,0:T(8,128)(2,1)} %constant.18.clone.hi, bf16[512,512]{1,0:T(8,128)(2,1)} %constant.19.clone.lo), custom_call_target="tpu_custom_call" | custom-call | tf_op jit(solution)/shard_map/y_pick/pallas_call | solution.py:471
  170.0 0.0 copy-start
  170.0 8.3 %interpolate.1 = f32[2,4,16,128]{3,2,1,0:T(8,128)} custom-call(f32[8,2,8,2,2,8,128]{6,5,4,3,2,1,0:T(8,128)} %bitcast.13, f32[2,16,512,128]{3,2,1,0:T(8,128)} %get-tuple-element.10.weights), custom_call_target="tpu_custom_call" | custom-call | tf_op jit(solution)/shard_map/interpolate/pallas_call | solution.py:511
  178.3 1.0 reshape.51
  179.3 0.3 reduce_sum.9
  179.6 0.1 copy.12
  179.7 0.0 copy-done
  179.7 0.1 iota_compare_fusion
  179.8 0.6 copy.13
  (1 shorter events, 0.0 us)
Async XLA Ops:
  170.0 9.7 %copy-start = (s32[16]{0:T(128)S(1)}, s32[16]{0:T(128)}, u32[]{:S(2)}) copy-start(s32[16]{0:T(128)} %param.15) | copy-start | bytes 196

commit v6 on v5

v6 whole, which is shorter than its diff:
```python
import functools
import math

import jax
import jax.numpy as jnp
import numpy as np
from jax import lax
from jax.experimental import pallas as pl
from jax.experimental.pallas import tpu as pltpu
from jax.sharding import PartitionSpec as P

NX, NY, NZ = 512, 256, 256
GX, GY = 8, 16
DEVS = GX * GY
F32, BF16 = jnp.float32, jnp.bfloat16
WIDE_VMEM = 62 * 2**20


def split_table(table):
    hi = table.astype(np.float32).astype(jnp.bfloat16)
    lo = (table - hi.astype(np.float64)).astype(np.float32).astype(jnp.bfloat16)
    return hi, lo


def angle(rows, columns, length):
    return (np.outer(rows, columns) % length) * (2.0 * math.pi / length)


def z_table():
    bz = np.arange(32).reshape(4, 1, 8)
    order = (np.arange(8)[None, :, None] + 8 * bz).reshape(-1)
    phase = angle(order, np.arange(NZ), NZ)
    scale = 1.0 / math.sqrt(NX * NY * NZ)
    return split_table(np.concatenate([np.cos(phase), np.sin(phase)], 1) * scale)


def x_table():
    phase = angle(np.arange(NX), np.arange(NX), NX)
    cos, sin = np.cos(phase), np.sin(phase)
    whole = np.zeros((2, NX, 2, NX))
    whole[0, :, 0], whole[1, :, 0] = cos, sin
    whole[0, :, 1], whole[1, :, 1] = -sin, cos
    whole = whole.reshape(2, 8, 64, 2, 64, 8).transpose(1, 0, 2, 5, 3, 4)
    return split_table(whole.reshape(1024, 1024))


def y_table():
    phase = angle(np.arange(NY), np.arange(NY), NY)
    cos, sin = np.cos(phase), np.sin(phase)
    whole = np.zeros((2, NY, 2, NY))
    whole[0, :, 0], whole[1, :, 0] = cos, sin
    whole[0, :, 1], whole[1, :, 1] = -sin, cos
    whole = whole.reshape(2, NY, 2, 32, 8).transpose(0, 1, 3, 2, 4)
    return split_table(whole.reshape(512, 512))


def halves(value):
    hi = value.astype(BF16)
    return hi, (value - hi.astype(F32)).astype(BF16)


def dot3(left, right, dims):
    def one(a, b):
        return lax.dot_general(a, b, (dims, ((), ())), preferred_element_type=F32)

    return one(left[0], right[0]) + (one(left[0], right[1]) + one(left[1], right[0]))


def z_pair(yp, c, image, hi, lo, sent):
    rows, swapped = [], []
    for k in range(2):
        at = pl.ds(2 * yp + k, 64, stride=16)
        re, im = (
            jnp.concatenate([image[half * 4 + c * 2 + q, at, :] for half in range(2)], 1)
            for q in range(2)
        )
        rows += [re, im]
        swapped += [im, -re]
    data = jnp.concatenate([jnp.concatenate(rows, 0), jnp.concatenate(swapped, 0)], 1)
    res = dot3((hi[...], lo[...]), halves(data), ((1,), (1,)))
    for k in range(2):
        part = res[:, k * 128 : (k + 1) * 128].reshape(4, 8, 8, 128)
        y = 2 * yp + k
        at = pl.multiple_of(c * 64 + y % 8 * 8, 8)
        for b in range(4):
            sent[y // 8 * 4 + b, :, pl.ds(at, 8), :] = part[b]


def hops(pairs, axis, size, sems):
    me = lax.axis_index(axis)
    src, dst = pairs
    made = []
    for r in range(1, size):
        to = (me + r) % size
        made.append(
            pltpu.make_async_remote_copy(
                src_ref=src(to),
                dst_ref=dst,
                send_sem=sems.at[0, r],
                recv_sem=sems.at[1, r],
                device_id={axis: to},
            )
        )
    return made


def own_rows(listed, slots, mine, gy):
    lists = pltpu.roll(listed[...].reshape(128, 128), (128 - gy) % 128, 1)
    row = lax.broadcasted_iota(jnp.int32, (128, 128), 0)
    first = row % 8 * 64 + row // 8 * 4
    for h in range(2):
        wanted = slots[h : h + 1, :]
        total = jnp.zeros((8, 128), jnp.int32)
        for k in range(4):
            column = jnp.broadcast_to(lists[:, 16 * k : 16 * k + 1], (128, 128))
            found = jnp.where(first + k == wanted, column, 0)
            for at in range(0, 128, 8):
                total += found[at : at + 8]
        for by in (4, 2, 1):
            total += pltpu.roll(total, by, 0)
        ids = total[:1]
        bz, by = ids % 32, ids // 32 % 32
        mine[h : h + 1, :] = bz * 2048 + by * 64 + ids // 1024 % 64


def turn_unit(block, turned):
    def one(n, carry):
        part = block[pl.ds(n, 128, stride=16), :].T
        for u in range(2):
            for v in range(8):
                at = (u * 8 + v) * 8
                turned[n, pl.ds(u * 64 + v, 8, stride=8), :] = part[at : at + 8]
        return carry

    lax.fori_loop(0, 16, one, 0)


def y_group(g, data, hi, lo, table):
    lane = lax.broadcasted_iota(jnp.int32, (64, 128), 1)

    def four(p, carry):
        rows = []
        for k in range(4):
            turned = data[pl.ds(4 * p + k, 256, stride=8), :].T
            rows.append(jnp.concatenate([turned[:64], turned[64:]], 1))
        res = dot3(halves(jnp.concatenate(rows, 0)), (hi[...], lo[...]), ((1,), (0,)))
        for k in range(4):
            bz = 8 * g + 4 * p + k
            for high in range(4):
                part = res[k * 64 : (k + 1) * 64, high * 128 : (high + 1) * 128]
                for low in range(8):
                    source = low * 16 + jnp.bitwise_and(lane, 15)
                    at = pl.multiple_of((bz * 32 + high * 8 + low) * 64, 64)
                    table[pl.ds(at, 64), :] = jnp.take_along_axis(part, source, axis=1)
        return carry

    lax.fori_loop(0, 2, four, 0)


def pick_group(to, gx, rows, table, raw):
    owners = [(gx + g) % GX for g in range(8)]

    def eight(t, carry):
        h, first = t // 16, t % 16 * 8
        for s in range(8):
            for g in range(8):
                lanes = slice(g * 16, g * 16 + 16)
                row = rows[to, owners[g], h, first + s]
                raw[pl.ds(t * 8 + s, 1), lanes] = table[pl.ds(row, 1), lanes]
        return carry

    lax.fori_loop(0, 32, eight, 0)


def spread_kernel(
    images, z_hi_in, z_lo_in, x_hi_in, x_lo_in, y_hi_in, y_lo_in, lists, slots, weights,
    out, turned_out,
    x_out, z_hi, z_lo, x_hi, x_lo, y_hi, y_lo, z_out, x_in, y_in, table, raw, rows_all, rows,
    near, near8, listed, mine, mine8, block, turned,
    load_sem, self_sem, send1, recv1, send2, recv2, send3, recv3,
    small1, small2, small3, small4, block_sem, turned_sem, rows_sem,
):
    gx, gy = lax.axis_index("gx"), lax.axis_index("gy")
    me = gx * GY + gy
    image = x_out
    loads = [
        pltpu.make_async_copy(src, dst, load_sem.at[i])
        for i, (src, dst) in enumerate(
            [(z_hi_in, z_hi), (z_lo_in, z_lo)]
            + [
                (images.at[c, q, :, pl.ds(half * 128, 128)], image.at[half * 4 + c * 2 + q])
                for c in range(2)
                for q in range(2)
                for half in range(2)
            ]
            + [(x_hi_in, x_hi), (x_lo_in, x_lo), (y_hi_in, y_hi), (y_lo_in, y_lo)]
        )
    ]
    for load in loads:
        load.start()

    barrier = pltpu.get_barrier_semaphore()
    for r in range(1, GX):
        pl.semaphore_signal(barrier, inc=1, device_id={"gx": (gx + r) % GX})
    for r in range(1, GY):
        pl.semaphore_signal(barrier, inc=1, device_id={"gy": (gy + r) % GY})
    pl.semaphore_wait(barrier, GX + GY - 2)

    def over_x(m, r):
        to = (gx + r) % GX
        return pltpu.make_async_remote_copy(
            src_ref=z_out.at[m, to],
            dst_ref=x_in.at[m, gx],
            send_sem=send1.at[m, r],
            recv_sem=recv1.at[m, r],
            device_id={"gx": to},
        )

    def part_y(m, b):
        return y_in.at[m % 4, pl.ds(pl.multiple_of(b * 128 + m // 4 * 64, 64), 64)]

    def over_y(m, r):
        to = (gy + r) % GY
        return pltpu.make_async_remote_copy(
            src_ref=x_out.at[m, pl.ds(pl.multiple_of(to * 64, 64), 64)],
            dst_ref=part_y(m, gy),
            send_sem=send2.at[m, r],
            recv_sem=recv2.at[m, r],
            device_id={"gy": to},
        )

    def own_y(m):
        src = x_out.at[m, pl.ds(pl.multiple_of(gy * 64, 64), 64)]
        return pltpu.make_async_copy(src, part_y(m, gy), self_sem.at[m])

    def picked(i, g):
        return z_out.at[g, i // 4, pl.ds(pl.multiple_of(i % 4 * 32, 32), 32)]

    def over_all(i, g):
        return pltpu.make_async_remote_copy(
            src_ref=picked(i, g),
            dst_ref=out.at[me],
            send_sem=send3.at[i, g],
            recv_sem=recv3.at[i, g],
            device_id={"gx": (gx + g) % GX, "gy": (gy + i) % GY},
        )

    hop1 = hops((lambda to: lists, near.at[gx]), "gx", GX, small1)
    hop2 = hops((lambda to: near8, listed.at[gy]), "gy", GY, small2)
    hop3 = hops((lambda to: mine, mine8.at[gx]), "gx", GX, small3)
    hop4 = hops((lambda to: mine8, rows_all.at[gy]), "gy", GY, small4)
    to_scalars = pltpu.make_async_copy(rows_all, rows, rows_sem)
    own = pltpu.make_async_copy(picked(0, 0), out.at[me], self_sem.at[8])

    def fetch(j, slot):
        src = weights.at[j // 4, :, pl.ds(j % 4 * 128, 128)]
        return pltpu.make_async_copy(src, block.at[slot], block_sem.at[slot])

    def put(j, slot):
        dst = turned_out.at[j // 4, :, pl.ds(j % 4 * 128, 128), :]
        return pltpu.make_async_copy(turned.at[slot], dst, turned_sem.at[slot])

    def z_half(half):
        for c in range(2):
            if half == 0:
                for load in loads[2 + 4 * c : 6 + 4 * c]:
                    load.wait()

            def pair(yp, carry):
                z_pair(yp + 4 * half, c, image, z_hi, z_lo, z_out)
                return carry

            lax.fori_loop(0, 4, pair, 0)

    def send_x(half):
        def one(m, carry):
            for r in range(1, GX):
                over_x(m, r).start()
            return carry

        lax.fori_loop(4 * half, 4 * half + 4, one, 0)

    for hop in hop1:
        hop.start()
    near[gx] = lists[...]
    for load in loads[:2]:
        load.wait()
    z_half(0)
    send_x(0)
    z_half(1)
    send_x(1)
    for slot in range(2):
        fetch(slot, slot).start()
    for hop in hop1:
        hop.wait()
    lane = lax.broadcasted_iota(jnp.int32, (1, 128), 1)
    for a in range(GX):
        kept = jnp.zeros((1, 128), jnp.int32)
        for k in range(4):
            moved = pltpu.roll(near[a, k : k + 1, :], (128 + 16 * k - 16 * gx) % 128, 1)
            kept = jnp.where(lane // 16 == k, moved, kept)
        near8[a : a + 1, :] = kept
    for hop in hop2:
        hop.start()
    listed[gy] = near8[...]
    for load in loads[10:]:
        load.wait()

    def chunk(m, carry):
        slot = m % 2
        fetch(m, slot).wait()

        @pl.when(m > 1)
        def _():
            put(m - 2, slot).wait()

        turn_unit(block.at[slot], turned.at[slot])
        put(m, slot).start()

        @pl.when(m < 6)
        def _():
            fetch(m + 2, slot).start()

        x_in[m, gx] = z_out[m, gx]
        for r in range(1, GX):
            over_x(m, r).wait_recv()
        both = jnp.concatenate([x_in[m, a] for a in range(8)], 1)
        res = dot3(halves(both), (x_hi[...], x_lo[...]), ((1,), (0,)))
        for c in range(2):
            for u in range(8):
                at = (c * 8 + u) * 64
                x_out[m, at : at + 64] = res[
                    c * 64 : (c + 1) * 64, u * 128 : (u + 1) * 128
                ]
        for r in range(1, GY):
            over_y(m, r).start()
        own_y(m).start()

        @pl.when(m == 2)
        def _():
            for hop in hop2:
                hop.wait()
            own_rows(listed, slots, mine, gy)
            for hop in hop3:
                hop.start()
            mine8[gx] = mine[...]

        @pl.when(m == 4)
        def _():
            for hop in hop3:
                hop.wait()
            for hop in hop4:
                hop.start()
            rows_all[gy] = mine8[...]

        return carry

    lax.fori_loop(0, 8, chunk, 0)

    def group_y(k, carry):
        for m in (k, k + 4):
            own_y(m).wait()
            for r in range(1, GY):
                over_y(m, r).wait_recv()
        y_group(k, y_in.at[k], y_hi, y_lo, table)
        return carry

    def sent_x(m, carry):
        for r in range(1, GX):
            over_x(m, r).wait_send()
        return carry

    lax.fori_loop(0, 8, sent_x, 0)
    for hop in hop4:
        hop.wait()
    to_scalars.start()
    for slot in range(2):
        put(6 + slot, slot).wait()
    lax.fori_loop(0, 4, group_y, 0)
    to_scalars.wait()

    def group(i, carry):
        to = (gy + i) % GY
        pick_group(to, gx, rows, table, raw)
        for h in range(2):
            turned_raw = raw[h * 128 : (h + 1) * 128, :].T
            for g in range(8):
                at = pl.multiple_of(i % 4 * 32 + h * 16, 16)
                part = turned_raw[g * 16 : (g + 1) * 16]
                z_out[g, i // 4, pl.ds(at, 16), :] = part

        @pl.when(i == 0)
        def _():
            own.start()

        @pl.when(i > 0)
        def _():
            over_all(i, 0).start()

        for g in range(1, 8):
            over_all(i, g).start()
        return carry

    lax.fori_loop(0, 16, group, 0)
    own.wait()

    def finish(m, carry):
        for r in range(1, GY):
            over_y(m, r).wait_send()
        return carry

    lax.fori_loop(0, 8, finish, 0)

    def finish_all(i, carry):
        @pl.when(i > 0)
        def _():
            over_all(i, 0).wait()

        for g in range(1, 8):
            over_all(i, g).wait()
        return carry

    lax.fori_loop(0, 16, finish_all, 0)


def spread(images, lists, slots, weights):
    tables = [jnp.asarray(t) for t in z_table() + x_table() + y_table()]
    hbm = pl.BlockSpec(memory_space=pltpu.HBM)
    inside = pl.BlockSpec(memory_space=pltpu.VMEM)
    dma = pltpu.SemaphoreType.DMA
    i32 = jnp.int32
    return pl.pallas_call(
        spread_kernel,
        out_shape=(
            jax.ShapeDtypeStruct((DEVS, 32, 128), F32),
            jax.ShapeDtypeStruct((2, 16, 512, 128), F32),
        ),
        in_specs=[hbm] * 7 + [inside] * 2 + [hbm],
        out_specs=(hbm,) * 2,
        scratch_shapes=[
            pltpu.VMEM((8, 1024, 128), F32),
            pltpu.VMEM((256, 512), BF16),
            pltpu.VMEM((256, 512), BF16),
            pltpu.VMEM((1024, 1024), BF16),
            pltpu.VMEM((1024, 1024), BF16),
            pltpu.VMEM((512, 512), BF16),
            pltpu.VMEM((512, 512), BF16),
            pltpu.VMEM((8, 8, 128, 128), F32),
            pltpu.VMEM((8, 8, 128, 128), F32),
            pltpu.VMEM((4, 2048, 128), F32),
            pltpu.VMEM((65536, 128), F32),
            pltpu.VMEM((256, 128), F32),
            pltpu.VMEM((GY, GX, 2, 128), i32),
            pltpu.SMEM((GY, GX, 2, 128), i32),
            pltpu.VMEM((GX, 4, 128), i32),
            pltpu.VMEM((GX, 128), i32),
            pltpu.VMEM((GY, GX, 128), i32),
            pltpu.VMEM((2, 128), i32),
            pltpu.VMEM((GX, 2, 128), i32),
            pltpu.VMEM((2, 2048, 128), F32),
            pltpu.VMEM((2, 16, 128, 128), F32),
            dma((14,)),
            dma((9,)),
            dma((8, GX)),
            dma((8, GX)),
            dma((8, GY)),
            dma((8, GY)),
            dma((16, 8)),
            dma((16, 8)),
            dma((2, GX)),
            dma((2, GY)),
            dma((2, GX)),
            dma((2, GY)),
            dma((2,)),
            dma((2,)),
            dma,
        ],
        compiler_params=pltpu.CompilerParams(
            vmem_limit_bytes=WIDE_VMEM, collective_id=0, has_side_effects=True
        ),
        name="spread",
    )(images, *tables, lists, slots, weights)


def sum_kernel(got, weights, out):
    def one(u, carry):
        sums = list(carry)
        for w in range(8):
            at = pl.multiple_of(u * 64 + w * 8, 8)
            factors = [weights[0, n, pl.ds(at, 8), :] for n in range(4)]
            for k in range(4):
                value = got[w, k // 2, u, 0, k % 2]
                for n in range(4):
                    sums[n * 4 + k] = sums[n * 4 + k] + factors[n] * value
        return tuple(sums)

    sums = lax.fori_loop(0, 8, one, (jnp.zeros((8, 128), F32),) * 16)
    rows = [jnp.sum(s, 0, keepdims=True) for s in sums]
    out[0, 0] = jnp.concatenate(rows, 0)


def interpolate(got, weights):
    return pl.pallas_call(
        sum_kernel,
        out_shape=jax.ShapeDtypeStruct((2, 4, 16, 128), F32),
        grid=(2, 4),
        in_specs=[
            pl.BlockSpec((8, 2, 8, 1, 2, 8, 128), lambda h, n: (0, 0, 0, h, 0, 0, 0)),
            pl.BlockSpec((1, 4, 512, 128), lambda h, n: (h, n, 0, 0)),
        ],
        out_specs=pl.BlockSpec((1, 1, 16, 128), lambda h, n: (h, n, 0, 0)),
        compiler_params=pltpu.CompilerParams(vmem_limit_bytes=WIDE_VMEM),
        name="interpolate",
    )(got, weights)


def local(coil_images, send_lists, seg_slots, weights, counts):
    lists = send_lists[0].T
    got, turned = spread(
        coil_images.reshape(2, 2, 1024, 256),
        lists,
        seg_slots.reshape(2, 128),
        weights.reshape(2, 2048, 512),
    )
    sums = interpolate(got.reshape(8, 2, 8, 2, 2, 8, 128), turned)
    sums = sums.reshape(2, 16, 2, 2, 8, 16).sum(-1)
    samples = sums.transpose(0, 4, 2, 3, 1).reshape(16, 2, 2, 16)
    live = jnp.arange(16, dtype=jnp.int32) < counts[:, None, None, None]
    return jnp.where(live, samples, 0.0)


def solution(mesh):
    placed = (
        P(None, None, "gx", "gy", None),
        P(("gx", "gy"), None, None),
        P(("gx", "gy"), None),
        P(("gx", "gy"), None, None, None),
        P(("gx", "gy")),
    )
    return jax.shard_map(
        local,
        mesh=mesh,
        in_specs=placed,
        out_specs=P(("gx", "gy"), None, None, None),
        check_vma=False,
    )
```

time: 181 us -> 190 us (1.050); the launches traced: 180 us -> 186 us
  Pallas kernels: 177 us -> 183 us
    pallas_call x2 -> x1, Pallas kernels: 169 us -> 175 us  [spread(): pl.pallas_call(spread_kernel, out_shape=(jax.ShapeDtypeStruct((DEVS, 32,...]
where the time goes in v6:
time: 190 us; the launch traced here: 186 us
  Pallas kernels  183 us (96%)
  local copies, waits for them, and re-layouts  3.09 us (2%)
    pallas_call x1, Pallas kernels, spread(): pl.pallas_call(spread_kernel, out_shape=(jax.ShapeDtypeStruct((DEVS, 32,...  175 us
    pallas_call x1, Pallas kernels, interpolate(): pl.pallas_call(sum_kernel, out_shape=jax.ShapeDtypeStruct((2, 4, 16, 128)...  8.32 us

profile of v6, /device:TPU:1, one launch (start us, length us, event | category | flops | bytes accessed | tf_op | source)
XLA Modules:
  0.0 186.4 jit_solution(11930525710416545655)
XLA Ops:
  0.0 1.3 reshape.40.slots
  1.3 174.6 %spread.1 = (f32[128,32,128]{2,1,0:T(8,128)}, f32[2,16,512,128]{3,2,1,0:T(8,128)}) custom-call(f32[2,2,1024,256]{3,2,1,0:T(8,128)} %bitcast.12, bf16[256,512]{1,0:T(8,128)(2,1)} %constant.14.clone.z_hi_in, bf16[256,512]{1,0:T(8,128)(2,1)} %constant.15.clone.z_lo_in, bf16[1024,1024]{1,0:T(8,128)(2,1)} %constant.16.clone.x_hi_in, ...), custom_call_target="tpu_custom_call" | custom-call | tf_op jit(solution)/shard_map/spread/pallas_call | solution.py:432
  176.0 0.0 copy-start
  176.0 8.3 %interpolate.1 = f32[2,4,16,128]{3,2,1,0:T(8,128)} custom-call(f32[8,2,8,2,2,8,128]{6,5,4,3,2,1,0:T(8,128)} %bitcast.13, f32[2,16,512,128]{3,2,1,0:T(8,128)} %get-tuple-element.8.weights), custom_call_target="tpu_custom_call" | custom-call | tf_op jit(solution)/shard_map/interpolate/pallas_call | solution.py:503
  184.3 1.0 reshape.43
  185.3 0.3 reduce_sum.9
  185.6 0.1 copy.12
  185.7 0.0 copy-done
  185.7 0.1 iota_compare_fusion
  185.8 0.6 copy.13
  (1 shorter events, 0.0 us)
Async XLA Ops:
  176.0 9.7 %copy-start = (s32[16]{0:T(128)S(1)}, s32[16]{0:T(128)}, u32[]{:S(2)}) copy-start(s32[16]{0:T(128)} %param.15) | copy-start | bytes 196

commit v7 on v6

--- a/solution.py
+++ b/solution.py
@@ -162,10 +162,11 @@
 
     def eight(t, carry):
         h, first = t // 16, t % 16 * 8
+        views = [rows.at[to, owners[g], h] for g in range(8)]
         for s in range(8):
             for g in range(8):
                 lanes = slice(g * 16, g * 16 + 16)
-                row = rows[to, owners[g], h, first + s]
+                row = views[g][first + s]
                 raw[pl.ds(t * 8 + s, 1), lanes] = table[pl.ds(row, 1), lanes]
         return carry
 
@@ -483,32 +484,44 @@
 
 
 def sum_kernel(got, weights, out):
-    def one(u, carry):
-        sums = list(carry)
-        for w in range(8):
-            at = pl.multiple_of(u * 64 + w * 8, 8)
-            factors = [weights[0, n, pl.ds(at, 8), :] for n in range(4)]
-            for k in range(4):
-                value = got[w, k // 2, u, 0, k % 2]
-                for n in range(4):
-                    sums[n * 4 + k] = sums[n * 4 + k] + factors[n] * value
-        return tuple(sums)
-
-    sums = lax.fori_loop(0, 8, one, (jnp.zeros((8, 128), F32),) * 16)
-    rows = [jnp.sum(s, 0, keepdims=True) for s in sums]
-    out[0, 0] = jnp.concatenate(rows, 0)
+    rows = []
+    for half in range(2):
+
+        def one(u, carry):
+            sums = list(carry)
+            for w in range(8):
+                at = pl.multiple_of(u * 64 + w * 8, 8)
+                factors = [weights[0, 4 * half + n, pl.ds(at, 8), :] for n in range(4)]
+                for k in range(4):
+                    value = got[w, k // 2, u, 0, k % 2]
+                    for n in range(4):
+                        sums[n * 4 + k] = sums[n * 4 + k] + factors[n] * value
+            return tuple(sums)
+
+        sums = lax.fori_loop(0, 8, one, (jnp.zeros((8, 128), F32),) * 16)
+        rows += [jnp.sum(s, 0, keepdims=True) for s in sums]
+    lane = lax.broadcasted_iota(jnp.int32, (8, 128), 1)
+    owner = lax.broadcasted_iota(jnp.int32, (8, 128), 0)
+    ones = jnp.where(lane // 16 == owner, 1.0, 0.0)
+    out[0, 0] = lax.dot_general(
+        ones,
+        jnp.concatenate(rows, 0),
+        (((1,), (1,)), ((), ())),
+        precision=lax.Precision.HIGHEST,
+        preferred_element_type=F32,
+    )
 
 
 def interpolate(got, weights):
     return pl.pallas_call(
         sum_kernel,
-        out_shape=jax.ShapeDtypeStruct((2, 4, 16, 128), F32),
-        grid=(2, 4),
+        out_shape=jax.ShapeDtypeStruct((2, 2, 8, 32), F32),
+        grid=(2, 2),
         in_specs=[
             pl.BlockSpec((8, 2, 8, 1, 2, 8, 128), lambda h, n: (0, 0, 0, h, 0, 0, 0)),
-            pl.BlockSpec((1, 4, 512, 128), lambda h, n: (h, n, 0, 0)),
+            pl.BlockSpec((1, 8, 512, 128), lambda h, n: (h, n, 0, 0)),
         ],
-        out_specs=pl.BlockSpec((1, 1, 16, 128), lambda h, n: (h, n, 0, 0)),
+        out_specs=pl.BlockSpec((1, 1, 8, 32), lambda h, n: (h, n, 0, 0)),
         compiler_params=pltpu.CompilerParams(vmem_limit_bytes=WIDE_VMEM),
         name="interpolate",
     )(got, weights)
@@ -523,8 +536,8 @@
         weights.reshape(2, 2048, 512),
     )
     sums = interpolate(got.reshape(8, 2, 8, 2, 2, 8, 128), turned)
-    sums = sums.reshape(2, 16, 2, 2, 8, 16).sum(-1)
-    samples = sums.transpose(0, 4, 2, 3, 1).reshape(16, 2, 2, 16)
+    samples = sums.reshape(2, 2, 8, 8, 2, 2).transpose(0, 2, 4, 5, 1, 3)
+    samples = samples.reshape(16, 2, 2, 16)
     live = jnp.arange(16, dtype=jnp.int32) < counts[:, None, None, None]
     return jnp.where(live, samples, 0.0)
 

time: 190 us -> 153 us (0.81); the launches traced: 186 us -> 153 us
  Pallas kernels: 183 us -> 150 us
    pallas_call x1, Pallas kernels: 175 us -> 143 us  [spread(): pl.pallas_call(spread_kernel, out_shape=(jax.ShapeDtypeStruct((DEVS, 32,...]
where the time goes in v7:
time: 153 us
  Pallas kernels  150 us (98%)
  local copies, waits for them, and re-layouts  2.98 us (2%)
    pallas_call x1, Pallas kernels, spread(): pl.pallas_call(spread_kernel, out_shape=(jax.ShapeDtypeStruct((DEVS, 32,...  143 us
    pallas_call x1, Pallas kernels, interpolate(): pl.pallas_call(sum_kernel, out_shape=jax.ShapeDtypeStruct((2, 2, 8, 32),...  6.92 us

profile of v7, /device:TPU:1, one launch (start us, length us, event | category | flops | bytes accessed | tf_op | source)
XLA Modules:
  0.0 153.2 jit_solution(17886558131840866346)
XLA Ops:
  0.0 1.3 reshape.40.slots
  1.3 143.2 %spread.1 = (f32[128,32,128]{2,1,0:T(8,128)}, f32[2,16,512,128]{3,2,1,0:T(8,128)}) custom-call(f32[2,2,1024,256]{3,2,1,0:T(8,128)} %bitcast.12, bf16[256,512]{1,0:T(8,128)(2,1)} %constant.14.clone.z_hi_in, bf16[256,512]{1,0:T(8,128)(2,1)} %constant.15.clone.z_lo_in, bf16[1024,1024]{1,0:T(8,128)(2,1)} %constant.16.clone.x_hi_in, ...), custom_call_target="tpu_custom_call" | custom-call | tf_op jit(solution)/shard_map/spread/pallas_call | solution.py:433
  144.5 0.0 copy-start
  144.5 6.9 %interpolate.1 = f32[2,2,8,32]{3,2,1,0:T(8,128)} custom-call(f32[8,2,8,2,2,8,128]{6,5,4,3,2,1,0:T(8,128)} %bitcast.13, f32[2,16,512,128]{3,2,1,0:T(8,128)} %get-tuple-element.8.weights), custom_call_target="tpu_custom_call" | custom-call | tf_op jit(solution)/shard_map/interpolate/pallas_call | solution.py:516
  151.4 0.8 copy.14
  152.2 0.1 copy.15
  152.3 0.1 reshape.44
  152.4 0.0 copy-done
  152.4 0.1 iota_compare_fusion
  152.5 0.6 copy.16
  (1 shorter events, 0.0 us)
Async XLA Ops:
  144.5 7.9 %copy-start = (s32[16]{0:T(128)S(1)}, s32[16]{0:T(128)}, u32[]{:S(2)}) copy-start(s32[16]{0:T(128)} %param.15) | copy-start | bytes 196

commit v8 on v7

--- a/solution.py
+++ b/solution.py
@@ -108,8 +108,14 @@
     lists = pltpu.roll(listed[...].reshape(128, 128), (128 - gy) % 128, 1)
     row = lax.broadcasted_iota(jnp.int32, (128, 128), 0)
     first = row % 8 * 64 + row // 8 * 4
+    lane = lax.broadcasted_iota(jnp.int32, (1, 128), 1)
     for h in range(2):
-        wanted = slots[h : h + 1, :]
+        wanted = jnp.zeros((1, 128), jnp.int32)
+        for at in range(8):
+            moved = slots[h * 8 + at : h * 8 + at + 1, :]
+            if at > 0:
+                moved = pltpu.roll(moved, 16 * at, 1)
+            wanted = jnp.where(lane // 16 == at, moved, wanted)
         total = jnp.zeros((8, 128), jnp.int32)
         for k in range(4):
             column = jnp.broadcast_to(lists[:, 16 * k : 16 * k + 1], (128, 128))
@@ -177,7 +183,7 @@
     images, z_hi_in, z_lo_in, x_hi_in, x_lo_in, y_hi_in, y_lo_in, lists, slots, weights,
     out, turned_out,
     x_out, z_hi, z_lo, x_hi, x_lo, y_hi, y_lo, z_out, x_in, y_in, table, raw, rows_all, rows,
-    near, near8, listed, mine, mine8, block, turned,
+    near, near8, listed, mine, mine8, wide, block, turned,
     load_sem, self_sem, send1, recv1, send2, recv2, send3, recv3,
     small1, small2, small3, small4, block_sem, turned_sem, rows_sem,
 ):
@@ -341,7 +347,9 @@
         def _():
             for hop in hop2:
                 hop.wait()
-            own_rows(listed, slots, mine, gy)
+            wide[...] = jnp.zeros((16, 128), jnp.int32)
+            wide[:, :16] = slots[...]
+            own_rows(listed, wide, mine, gy)
             for hop in hop3:
                 hop.start()
             mine8[gx] = mine[...]
@@ -458,6 +466,7 @@
             pltpu.VMEM((GY, GX, 128), i32),
             pltpu.VMEM((2, 128), i32),
             pltpu.VMEM((GX, 2, 128), i32),
+            pltpu.VMEM((16, 128), i32),
             pltpu.VMEM((2, 2048, 128), F32),
             pltpu.VMEM((2, 16, 128, 128), F32),
             dma((14,)),
@@ -532,7 +541,7 @@
     got, turned = spread(
         coil_images.reshape(2, 2, 1024, 256),
         lists,
-        seg_slots.reshape(2, 128),
+        seg_slots,
         weights.reshape(2, 2048, 512),
     )
     sums = interpolate(got.reshape(8, 2, 8, 2, 2, 8, 128), turned)

time: 153 us -> 152 us (level)
  no operation moved by 1% of the time
where the time goes in v8:
time: 152 us
  Pallas kernels  150 us (99%)
  local copies, waits for them, and re-layouts  1.64 us (1%)
    pallas_call x1, Pallas kernels, spread(): pl.pallas_call(spread_kernel, out_shape=(jax.ShapeDtypeStruct((DEVS, 32,...  143 us
    pallas_call x1, Pallas kernels, interpolate(): pl.pallas_call(sum_kernel, out_shape=jax.ShapeDtypeStruct((2, 2, 8, 32),...  6.92 us

profile of v8, /device:TPU:1, one launch (start us, length us, event | category | flops | bytes accessed | tf_op | source)
XLA Modules:
  0.0 151.7 jit_solution(17067869976304522946)
XLA Ops:
  0.0 143.0 %spread.1 = (f32[128,32,128]{2,1,0:T(8,128)}, f32[2,16,512,128]{3,2,1,0:T(8,128)}) custom-call(f32[2,2,1024,256]{3,2,1,0:T(8,128)} %bitcast.12, bf16[256,512]{1,0:T(8,128)(2,1)} %constant.14.clone.z_hi_in, bf16[256,512]{1,0:T(8,128)(2,1)} %constant.15.clone.z_lo_in, bf16[1024,1024]{1,0:T(8,128)(2,1)} %constant.16.clone.x_hi_in, ...), custom_call_target="tpu_custom_call" | custom-call | tf_op jit(solution)/shard_map/spread/pallas_call | solution.py:441
  143.0 0.0 copy-start
  143.0 6.9 %interpolate.1 = f32[2,2,8,32]{3,2,1,0:T(8,128)} custom-call(f32[8,2,8,2,2,8,128]{6,5,4,3,2,1,0:T(8,128)} %bitcast.13, f32[2,16,512,128]{3,2,1,0:T(8,128)} %get-tuple-element.8.weights), custom_call_target="tpu_custom_call" | custom-call | tf_op jit(solution)/shard_map/interpolate/pallas_call | solution.py:525
  150.0 0.8 copy.14
  150.8 0.1 copy.15
  150.9 0.1 reshape.40
  151.0 0.0 copy-done
  151.0 0.1 iota_compare_fusion
  151.1 0.6 copy.16
  (1 shorter events, 0.0 us)
Async XLA Ops:
  143.0 7.9 %copy-start = (s32[16]{0:T(128)S(1)}, s32[16]{0:T(128)}, u32[]{:S(2)}) copy-start(s32[16]{0:T(128)} %param.15) | copy-start | bytes 196
